TPU v7x, 32 devices: a whole 2x2x4 slice. The times are simulated.
32 devices in a mesh: dp: 2 (over y), row: 4 (over x, core), col: 4 (over z).
Axes of the slice: x: 2, y: 2, z: 4, core: 2. Of those that a mesh axis runs over, the one named last changes fastest.
Arguments:
- tokens: bfloat16 [8192, 768], P(('dp', 'col', 'row')), may hold values from -6 to 6
- cotangent: bfloat16 [8192, 768], P(('dp', 'col', 'row')), may hold values from -6 to 6
- lengths: int32 [2], P('dp'), may hold values from 1024 to 4096, as said below
- query_weight: float32 [768, 768], P(('row', 'col')), may hold values from -0.21875 to 0.21875
- key_weight: float32 [768, 768], P(('row', 'col')), may hold values from -0.21875 to 0.21875
- value_weight: float32 [768, 768], P(('row', 'col')), may hold values from -0.21875 to 0.21875
- query_bias: float32 [768], P('col'), may hold values from -3 to 3
- value_bias: float32 [768], P('col'), may hold values from -0.1875 to 0.1875
- out_weight: float32 [768, 768], P(('col', 'row')), may hold values from -6 to 6
- out_bias: float32 [768], P('row'), may hold values from -1.75 to 1.75
- norm1_gain: float32 [768], P('row'), may hold values from 0.5 to 1.5
- norm1_shift: float32 [768], P('row'), may hold values from -1.75 to 1.75
- up_weight: float32 [768, 3072], P('row', 'col'), may hold values from -0.21875 to 0.21875
- up_bias: float32 [3072], P('col'), may hold values from -3 to 3
- down_weight: float32 [3072, 768], P(('col', 'row')), may hold values from -0.109375 to 0.109375
- down_bias: float32 [768], P('row'), may hold values from -1.75 to 1.75
- norm2_gain: float32 [768], P('row'), may hold values from 0.5 to 1.5
- norm2_shift: float32 [768], P('row'), may hold values from -1.75 to 1.75
Outputs:
- output: bfloat16 [8192, 768], P(('dp', 'col', 'row'))
- grad_tokens: float32 [8192, 768], P(('dp', 'col', 'row'))
- grad_query_weight: float32 [768, 768], P(('row', 'col'))
- grad_key_weight: float32 [768, 768], P(('row', 'col'))
- grad_value_weight: float32 [768, 768], P(('row', 'col'))
- grad_query_bias: float32 [768], P('col')
- grad_value_bias: float32 [768], P('col')
- grad_out_weight: float32 [768, 768], P(('col', 'row'))
- grad_out_bias: float32 [768], P('row')
- grad_norm1_gain: float32 [768], P('row')
- grad_norm1_shift: float32 [768], P('row')
- grad_up_weight: float32 [768, 3072], P('row', 'col')
- grad_up_bias: float32 [3072], P('col')
- grad_down_weight: float32 [3072, 768], P(('col', 'row'))
- grad_down_bias: float32 [768], P('row')
- grad_norm2_gain: float32 [768], P('row')
- grad_norm2_shift: float32 [768], P('row')
Inputs may be any that keep to these rules, and one draw needn't show every extreme that they name: `lengths`: one sequence is exactly 4096 long.
All inputs are finite; a program needn't handle non-finite values.
Results may differ from a plain program's by a relative error of at most 0.024.
Values may be sent and summed in bfloat16 or wider, within the bound.
No kernel may reach another device: no remote copies, remote signals or barrier semaphores. Data moves between devices by JAX's collectives and lax.ppermute only.
A program may use at most 256 MiB of HBM per device.

v0:
```python
import math

import jax
import jax.numpy as jnp
from jax import lax
from jax.sharding import PartitionSpec as P

D = 768
HD = 64


eps_norm = 1e-05


def matmul(left_mat, right_mat):
    return jnp.dot(left_mat, right_mat, preferred_element_type=jnp.float32)


def matmul_tn(left_mat, right_mat):
    return lax.dot_general(
        left_mat, right_mat, (((0,), (0,)), ((), ())), preferred_element_type=jnp.float32
    )


def matmul_nt(left_mat, right_mat):
    return lax.dot_general(
        left_mat, right_mat, (((1,), (1,)), ((), ())), preferred_element_type=jnp.float32
    )


def across_cols(shard_in):
    return lax.all_gather(shard_in, "col", axis=0, tiled=True)


def col_sums(shard_in):
    return lax.psum_scatter(
        shard_in.astype(jnp.bfloat16), "col", scatter_dimension=0, tiled=True
    ).astype(jnp.float32)


def row_gather(shard_in):
    return lax.all_gather(shard_in, "row", axis=0, tiled=True)


def row_reduce(shard_in):
    return lax.psum_scatter(shard_in, "row", scatter_dimension=0, tiled=True)


def row_totals(total_one, total_two):
    return lax.psum((total_one, total_two), "row")


def place_block(vector, total, block_index):
    empty = jnp.zeros((total,), jnp.float32)
    return lax.dynamic_update_slice_in_dim(empty, vector, block_index * vector.shape[0], 0)


def norm_forward(resid, norm_gain, norm_shift):
    total_one, total_two = row_totals(jnp.sum(resid, axis=1), jnp.sum(resid * resid, axis=1))
    row_mean = total_one / D
    row_var = total_two / D - row_mean * row_mean
    inv_std = lax.rsqrt(row_var + eps_norm)
    normal_rows = (resid - row_mean[:, None]) * inv_std[:, None]
    return (normal_rows * norm_gain + norm_shift, normal_rows, inv_std)


def norm_backward(grad_out, normal_rows, inv_std, norm_gain):
    scaled = grad_out * norm_gain
    total_one, total_two = row_totals(
        jnp.sum(scaled, axis=1), jnp.sum(scaled * normal_rows, axis=1)
    )
    grad_in = inv_std[:, None] * (
        scaled - total_one[:, None] / D - normal_rows * (total_two[:, None] / D)
    )
    return (grad_in, jnp.sum(grad_out * normal_rows, axis=0), jnp.sum(grad_out, axis=0))


def head_forward(queries, key_rows, values, key_ok, score_scale):
    scores = jnp.where(key_ok[None, :], matmul_nt(queries, key_rows) * score_scale, -1e30)
    peak_score = jnp.max(scores, axis=1, keepdims=True)
    exp_scores = jnp.exp(scores - peak_score)
    row_total = jnp.sum(exp_scores, axis=1, keepdims=True)
    attn_low = (exp_scores / row_total).astype(jnp.bfloat16)
    return (matmul(attn_low, values), peak_score[:, 0] + jnp.log(row_total[:, 0]))


def head_backward(queries, key_rows, values, grad_mixed, log_total, key_ok, score_scale):
    scores = jnp.where(key_ok[None, :], matmul_nt(queries, key_rows) * score_scale, -1e30)
    attn_weights = jnp.exp(scores - log_total[:, None])
    grad_attn = matmul_nt(grad_mixed, values)
    inner_sum = jnp.sum(attn_weights * grad_attn, axis=1, keepdims=True)
    grad_scores = (attn_weights * (grad_attn - inner_sum)).astype(jnp.bfloat16)
    grad_queries = matmul(grad_scores, key_rows) * score_scale
    grad_keys = matmul_tn(grad_scores, queries) * score_scale
    grad_values = matmul_tn(attn_weights.astype(jnp.bfloat16), grad_mixed)
    return (grad_queries, grad_keys, grad_values)


def gelu_exact(preact):
    return jax.nn.gelu(preact, approximate=False)


def per_device(
    tokens,
    cotangent,
    lengths,
    query_weight,
    key_weight,
    value_weight,
    query_bias,
    value_bias,
    out_weight,
    out_bias,
    norm1_gain,
    norm1_shift,
    up_weight,
    up_bias,
    down_weight,
    down_bias,
    norm2_gain,
    norm2_shift,
):
    tokens_block, cot_block = (
        lax.all_to_all(tokens, "row", split_axis=1, concat_axis=0, tiled=True),
        lax.all_to_all(cotangent, "row", split_axis=1, concat_axis=0, tiled=True),
    )
    quarter = tokens_block.shape[0]
    row_count = lax.axis_size("row")
    col_count = lax.axis_size("col")
    seq_len = quarter * col_count
    length = lengths[0]
    col_index = lax.axis_index("col")
    row_index = lax.axis_index("row")
    col_pos = col_index * quarter + jnp.arange(quarter, dtype=jnp.int32)
    valid_rows = (col_pos < length).astype(jnp.float32)[:, None]
    key_ok = jnp.arange(seq_len, dtype=jnp.int32) < length
    score_scale = 1.0 / math.sqrt(HD)
    feat_width = norm1_gain.shape[0]
    unit_width = up_bias.shape[0]
    query_rows, key_rows_w, value_rows = (
        lax.all_gather(query_weight.astype(jnp.bfloat16), "col", axis=0, tiled=True),
        lax.all_gather(key_weight.astype(jnp.bfloat16), "col", axis=0, tiled=True),
        lax.all_gather(value_weight.astype(jnp.bfloat16), "col", axis=0, tiled=True),
    )
    head_cols = query_rows.shape[1] // col_count
    query_low = lax.dynamic_slice_in_dim(query_rows, col_index * head_cols, head_cols, 1)
    key_low = lax.dynamic_slice_in_dim(key_rows_w, col_index * head_cols, head_cols, 1)
    value_low = lax.dynamic_slice_in_dim(value_rows, col_index * head_cols, head_cols, 1)
    out_rows, down_rows = (
        lax.all_gather(out_weight.astype(jnp.bfloat16), "row", axis=0, tiled=True),
        lax.all_gather(down_weight.astype(jnp.bfloat16), "row", axis=0, tiled=True),
    )
    feat_cols = out_rows.shape[1] // row_count
    out_low = lax.dynamic_slice_in_dim(out_rows, row_index * feat_cols, feat_cols, 1)
    down_low = lax.dynamic_slice_in_dim(down_rows, row_index * feat_cols, feat_cols, 1)
    up_low = up_weight.astype(jnp.bfloat16)
    head_count = head_cols // HD
    inputs_all = across_cols(tokens_block)
    joined = jnp.concatenate([query_low, key_low, value_low], axis=1)
    partials = row_reduce(matmul(inputs_all, joined))
    queries = (partials[:, :head_cols] + query_bias).astype(jnp.bfloat16)
    kv_bias = jnp.concatenate([jnp.zeros_like(value_bias), value_bias])
    kv_low = (partials[:, head_cols:] + kv_bias).astype(jnp.bfloat16)
    kv_all = row_gather(kv_low)
    keys_all = kv_all[:, :head_cols]
    values_all = kv_all[:, head_cols:]
    head_outs = []
    head_totals = []
    for head_index in range(head_count):
        first_col = head_index * HD
        head_out, log_total = head_forward(
            queries[:, first_col : first_col + HD],
            keys_all[:, first_col : first_col + HD],
            values_all[:, first_col : first_col + HD],
            key_ok,
            score_scale,
        )
        head_outs.append(head_out)
        head_totals.append(log_total)
    mixed = jnp.concatenate(head_outs, axis=1).astype(jnp.bfloat16)
    mixed_all = row_gather(mixed)
    attended = col_sums(matmul(mixed_all, out_low)) + out_bias
    hidden, normal_one, inv_one = norm_forward(
        tokens_block.astype(jnp.float32) + attended, norm1_gain, norm1_shift
    )
    hidden_low = hidden.astype(jnp.bfloat16)
    hidden_all = across_cols(hidden_low)
    preact = row_reduce(matmul(hidden_all, up_low)) + up_bias
    active = gelu_exact(preact).astype(jnp.bfloat16)
    active_all = row_gather(active)
    branch = col_sums(matmul(active_all, down_low)) + down_bias
    normed, normal_two, inv_two = norm_forward(hidden + branch, norm2_gain, norm2_shift)
    output_block = (normed * valid_rows).astype(jnp.bfloat16)
    grad_y = cot_block.astype(jnp.float32) * valid_rows
    grad_resid2, grad_norm2_gain, grad_norm2_shift = norm_backward(
        grad_y, normal_two, inv_two, norm2_gain
    )
    grad_branch_low = grad_resid2.astype(jnp.bfloat16)
    grad_down_bias_part = jnp.sum(grad_branch_low, axis=0, dtype=jnp.float32)
    gelu_value, gelu_pull = jax.vjp(gelu_exact, preact)
    grad_branch_all = across_cols(grad_branch_low)
    grad_down_weight = matmul_tn(active_all, grad_branch_all)
    grad_active = row_reduce(matmul_nt(grad_branch_all, down_low))
    grad_preact = gelu_pull(grad_active)[0].astype(jnp.bfloat16)
    grad_preact_all = row_gather(grad_preact)
    grad_up_weight = matmul_tn(hidden_all, grad_preact_all)
    grad_up_bias_part = place_block(
        jnp.sum(grad_preact, axis=0, dtype=jnp.float32), unit_width * col_count, col_index
    )
    grad_hidden = col_sums(matmul_nt(grad_preact_all, up_low)) + grad_resid2
    grad_resid1, grad_norm1_gain, grad_norm1_shift = norm_backward(
        grad_hidden, normal_one, inv_one, norm1_gain
    )
    grad_attended_all = across_cols(grad_resid1.astype(jnp.bfloat16))
    grad_out_weight = matmul_tn(mixed_all, grad_attended_all)
    grad_out_bias = jnp.sum(grad_attended_all, axis=0, dtype=jnp.float32)
    grad_mixed = row_reduce(matmul_nt(grad_attended_all, out_low)).astype(jnp.bfloat16)
    query_grads = []
    key_grads = []
    value_grads = []
    for head_index in range(head_count):
        first_col = head_index * HD
        grad_q_head, grad_k_head, grad_v_head = head_backward(
            queries[:, first_col : first_col + HD],
            keys_all[:, first_col : first_col + HD],
            values_all[:, first_col : first_col + HD],
            grad_mixed[:, first_col : first_col + HD],
            head_totals[head_index],
            key_ok,
            score_scale,
        )
        query_grads.append(grad_q_head)
        key_grads.append(grad_k_head)
        value_grads.append(grad_v_head)
    grad_queries = jnp.concatenate(query_grads, axis=1).astype(jnp.bfloat16)
    grad_kv = row_reduce(jnp.concatenate(key_grads + value_grads, axis=1))
    grad_qkv_all = row_gather(jnp.concatenate([grad_queries, grad_kv.astype(jnp.bfloat16)], axis=1))
    grad_q_all = grad_qkv_all[:, :head_cols]
    grad_k_all = grad_qkv_all[:, head_cols : 2 * head_cols]
    grad_v_all = grad_qkv_all[:, 2 * head_cols :]
    grad_query_weight = matmul_tn(inputs_all, grad_q_all)
    grad_key_weight = matmul_tn(inputs_all, grad_k_all)
    grad_value_weight = matmul_tn(inputs_all, grad_v_all)
    grad_query_bias = jnp.sum(grad_q_all, axis=0, dtype=jnp.float32)
    grad_value_bias = jnp.sum(grad_v_all, axis=0, dtype=jnp.float32)
    grad_back = (
        matmul_nt(grad_q_all, query_low)
        + matmul_nt(grad_k_all, key_low)
        + matmul_nt(grad_v_all, value_low)
    )
    grad_tokens_block = grad_resid1 + col_sums(grad_back)
    (
        grad_query_weight,
        grad_key_weight,
        grad_value_weight,
        grad_out_weight,
        grad_up_weight,
        grad_down_weight,
        grad_query_bias,
        grad_value_bias,
        grad_out_bias,
    ) = (
        lax.psum(grad_query_weight.astype(jnp.bfloat16), "dp").astype(jnp.float32),
        lax.psum(grad_key_weight.astype(jnp.bfloat16), "dp").astype(jnp.float32),
        lax.psum(grad_value_weight.astype(jnp.bfloat16), "dp").astype(jnp.float32),
        lax.psum(grad_out_weight.astype(jnp.bfloat16), "dp").astype(jnp.float32),
        lax.psum(grad_up_weight.astype(jnp.bfloat16), "dp").astype(jnp.float32),
        lax.psum(grad_down_weight.astype(jnp.bfloat16), "dp").astype(jnp.float32),
        lax.psum(grad_query_bias.astype(jnp.bfloat16), "dp").astype(jnp.float32),
        lax.psum(grad_value_bias.astype(jnp.bfloat16), "dp").astype(jnp.float32),
        lax.psum(grad_out_bias.astype(jnp.bfloat16), "dp").astype(jnp.float32),
    )
    full_width = feat_width * row_count
    sum_n1_gain, sum_n1_shift, sum_n2_gain, sum_n2_shift, sum_up_bias, sum_down_bias = lax.psum(
        (
            place_block(grad_norm1_gain, full_width, row_index),
            place_block(grad_norm1_shift, full_width, row_index),
            place_block(grad_norm2_gain, full_width, row_index),
            place_block(grad_norm2_shift, full_width, row_index),
            grad_up_bias_part,
            place_block(grad_down_bias_part, full_width, row_index),
        ),
        ("dp", "row", "col"),
    )
    grad_norm1_gain = lax.dynamic_slice_in_dim(sum_n1_gain, row_index * feat_width, feat_width, 0)
    grad_norm1_shift = lax.dynamic_slice_in_dim(sum_n1_shift, row_index * feat_width, feat_width, 0)
    grad_norm2_gain = lax.dynamic_slice_in_dim(sum_n2_gain, row_index * feat_width, feat_width, 0)
    grad_norm2_shift = lax.dynamic_slice_in_dim(sum_n2_shift, row_index * feat_width, feat_width, 0)
    grad_down_bias = lax.dynamic_slice_in_dim(sum_down_bias, row_index * feat_width, feat_width, 0)
    grad_up_bias = lax.dynamic_slice_in_dim(sum_up_bias, col_index * unit_width, unit_width, 0)
    grad_query_weight, grad_key_weight, grad_value_weight = (
        lax.all_to_all(
            grad_query_weight.astype(jnp.bfloat16), "col", split_axis=0, concat_axis=1, tiled=True
        ).astype(grad_query_weight.dtype),
        lax.all_to_all(
            grad_key_weight.astype(jnp.bfloat16), "col", split_axis=0, concat_axis=1, tiled=True
        ).astype(grad_key_weight.dtype),
        lax.all_to_all(
            grad_value_weight.astype(jnp.bfloat16), "col", split_axis=0, concat_axis=1, tiled=True
        ).astype(grad_value_weight.dtype),
    )
    grad_out_weight, grad_down_weight = (
        lax.all_to_all(
            grad_out_weight.astype(jnp.bfloat16), "row", split_axis=0, concat_axis=1, tiled=True
        ).astype(grad_out_weight.dtype),
        lax.all_to_all(
            grad_down_weight.astype(jnp.bfloat16), "row", split_axis=0, concat_axis=1, tiled=True
        ).astype(grad_down_weight.dtype),
    )
    output_wide, grad_tokens = (
        lax.all_to_all(
            output_block.astype(jnp.float32).astype(jnp.bfloat16),
            "row",
            split_axis=0,
            concat_axis=1,
            tiled=True,
        ).astype(jnp.float32),
        lax.all_to_all(
            grad_tokens_block.astype(jnp.bfloat16), "row", split_axis=0, concat_axis=1, tiled=True
        ).astype(grad_tokens_block.dtype),
    )
    output = output_wide.astype(jnp.bfloat16)
    return (
        output,
        grad_tokens,
        grad_query_weight,
        grad_key_weight,
        grad_value_weight,
        grad_query_bias,
        grad_value_bias,
        grad_out_weight,
        grad_out_bias,
        grad_norm1_gain,
        grad_norm1_shift,
        grad_up_weight,
        grad_up_bias,
        grad_down_weight,
        grad_down_bias,
        grad_norm2_gain,
        grad_norm2_shift,
    )


def solution(mesh):
    placed = (
        P(("dp", "col", "row"), None),
        P(("dp", "col", "row"), None),
        P("dp"),
        P(("row", "col"), None),
        P(("row", "col"), None),
        P(("row", "col"), None),
        P("col"),
        P("col"),
        P(("col", "row"), None),
        P("row"),
        P("row"),
        P("row"),
        P("row", "col"),
        P("col"),
        P(("col", "row"), None),
        P("row"),
        P("row"),
        P("row"),
    )
    return jax.shard_map(
        per_device,
        mesh=mesh,
        in_specs=placed,
        out_specs=(
            P(("dp", "col", "row"), None),
            P(("dp", "col", "row"), None),
            P(("row", "col"), None),
            P(("row", "col"), None),
            P(("row", "col"), None),
            P("col"),
            P("col"),
            P(("col", "row"), None),
            P("row"),
            P("row"),
            P("row"),
            P("row", "col"),
            P("col"),
            P(("col", "row"), None),
            P("row"),
            P("row"),
            P("row"),
        ),
        check_vma=False,
    )
```

profile of v0, /device:TPU:0, one launch (start us, length us, event | category | flops | bytes accessed | tf_op | source)
XLA Modules:
  0.0 1307.6 jit_solution(10679352518965303200)
XLA Ops:
  8.4 11.5 all_to_all.129
  22.6 15.6 %all_gather.44 = bf16[192,768]{1,0:T(8,128)(2,1)S(1)} all-gather(bf16[48,768]{1,0:T(8,128)(2,1)S(1)} %convert_element_type.253), channel_id=1, replica_groups=mesh['dp'=2,'row'=4,'col'=4] {'col'}, dimensions={0}, use_global_device_ids=true | all-gather | bytes 368640 | tf_op jit(solution)/shard_map/all_gather | solution.py:143
  38.3 17.3 %all_gather.43 = bf16[192,768]{1,0:T(8,128)(2,1)S(1)} all-gather(bf16[48,768]{1,0:T(8,128)(2,1)S(1)} %convert_element_type.252), channel_id=1, replica_groups=mesh['dp'=2,'row'=4,'col'=4] {'col'}, dimensions={0}, use_global_device_ids=true | all-gather | bytes 368640 | tf_op jit(solution)/shard_map/all_gather | solution.py:142
  55.6 16.1 %all_gather.42 = bf16[192,768]{1,0:T(8,128)(2,1)S(1)} all-gather(bf16[48,768]{1,0:T(8,128)(2,1)S(1)} %convert_element_type.251), channel_id=1, replica_groups=mesh['dp'=2,'row'=4,'col'=4] {'col'}, dimensions={0}, use_global_device_ids=true | all-gather | bytes 368640 | tf_op jit(solution)/shard_map/all_gather | solution.py:141
  72.1 6.6 convolution_bitcast_fusion
  79.5 77.9 %reduce-scatter.10.cloned.1.call-done = f32[1024,576]{0,1:T(8,128)} async-done(((f32[4096,576]{0,1:T(8,128)}), f32[1024,576]{0,1:T(8,128)}) %reduce-scatter.10.cloned.1.call-update) | async-done | bytes 2359312 | tf_op jit(solution)/shard_map/reduce_scatter | solution.py:46
  161.9 26.6 %all-gather.13.cloned.1.call-done = bf16[4096,384]{0,1:T(8,128)(2,1)} async-done(((bf16[1024,384]{0,1:T(8,128)(2,1)}), bf16[4096,384]{0,1:T(8,128)(2,1)}) %all-gather.13.cloned.1.call-update) | async-done | bytes 3145744 | tf_op jit(solution)/shard_map/all_gather | solution.py:42
  188.5 8.2 fusion.123
  196.7 8.1 fusion.2
  204.8 8.2 fusion.124
  213.0 8.1 fusion.1
  221.1 8.2 fusion.125
  229.4 8.2 fusion
  237.7 8.1 fusion.51
  247.2 4.5 fusion.52
  251.7 7.7 fusion.53
  260.4 5.9 all_gather.48
  266.3 13.8 %all-gather.15.cloned.1.call-done = bf16[4096,192]{0,1:T(8,128)(2,1)} async-done(((bf16[1024,192]{0,1:T(8,128)(2,1)}), bf16[4096,192]{0,1:T(8,128)(2,1)}) %all-gather.15.cloned.1.call-update) | async-done | bytes 1572880 | tf_op jit(solution)/shard_map/all_gather | solution.py:42
  283.5 35.4 %reduce-scatter.12.cloned.1.call-done = bf16[1024,192]{0,1:T(8,128)(2,1)} async-done(((bf16[4096,192]{0,1:T(8,128)(2,1)}), bf16[1024,192]{0,1:T(8,128)(2,1)}) %reduce-scatter.12.cloned.1.call-update) | async-done | bytes 393232 | tf_op jit(solution)/shard_map/reduce_scatter | solution.py:36
  320.1 6.5 all-reduce.5
  328.8 35.8 %all-gather.17.cloned.1.call-done = bf16[4096,192]{0,1:T(8,128)(2,1)} async-done(((bf16[1024,192]{0,1:T(8,128)(2,1)}), bf16[4096,192]{0,1:T(8,128)(2,1)}) %all-gather.17.cloned.1.call-update) | async-done | bytes 1572880 | tf_op jit(solution)/shard_map/all_gather | solution.py:32
  364.6 7.8 fusion.94
  374.2 96.2 %reduce-scatter.14.cloned.1.call-done = f32[1024,768]{1,0:T(8,128)} async-done(((f32[4096,768]{1,0:T(8,128)}), f32[1024,768]{1,0:T(8,128)}) %reduce-scatter.14.cloned.1.call-update) | async-done | bytes 3145744 | tf_op jit(solution)/shard_map/reduce_scatter | solution.py:46
  470.5 9.1 multiply_convert_fusion.3
  480.1 10.0 all-gather.21.cloned.1.call-done
  490.1 48.0 %all-gather.19.cloned.1.call-done = bf16[4096,768]{1,0:T(8,128)(2,1)} async-done(((bf16[1024,768]{1,0:T(8,128)(2,1)}), bf16[4096,768]{1,0:T(8,128)(2,1)}) %all-gather.19.cloned.1.call-update) | async-done | bytes 6291472 | tf_op jit(solution)/shard_map/all_gather | solution.py:42
  538.1 6.3 convolution_convert_fusion.1
  548.9 7.3 all-to-all-done.2
  557.1 22.7 %reduce-scatter.16.cloned.1.call-done = bf16[1024,192]{0,1:T(8,128)(2,1)} async-done(((bf16[4096,192]{0,1:T(8,128)(2,1)}), bf16[1024,192]{0,1:T(8,128)(2,1)}) %reduce-scatter.16.cloned.1.call-update) | async-done | bytes 393232 | tf_op jit(solution)/shard_map/reduce_scatter | solution.py:36
  581.3 6.5 all-reduce.4
  588.7 5.9 all-reduce.3
  596.4 35.9 %all-gather.23.cloned.1.call-done = bf16[4096,192]{0,1:T(8,128)(2,1)} async-done(((bf16[1024,192]{0,1:T(8,128)(2,1)}), bf16[4096,192]{0,1:T(8,128)(2,1)}) %all-gather.23.cloned.1.call-update) | async-done | bytes 1572880 | tf_op jit(solution)/shard_map/all_gather | solution.py:32
  632.2 8.1 fusion.85
  640.4 98.0 %reduce-scatter.18.cloned.1.call-done = f32[1024,768]{1,0:T(8,128)} async-done(((f32[4096,768]{1,0:T(8,128)}), f32[1024,768]{1,0:T(8,128)}) %reduce-scatter.18.cloned.1.call-update) | async-done | bytes 3145744 | tf_op jit(solution)/shard_map/reduce_scatter | solution.py:46
  738.4 7.0 convert_reduce_fusion
  745.5 46.5 %all-gather.25.cloned.1.call-done = bf16[4096,768]{1,0:T(8,128)(2,1)} async-done(((bf16[1024,768]{1,0:T(8,128)(2,1)}), bf16[4096,768]{1,0:T(8,128)(2,1)}) %all-gather.25.cloned.1.call-update) | async-done | bytes 6291472 | tf_op jit(solution)/shard_map/all_gather | solution.py:42
  792.0 6.1 convolution_convert_fusion
  798.2 35.4 %reduce-scatter.20.cloned.1.call-done = bf16[1024,192]{0,1:T(8,128)(2,1)} async-done(((bf16[4096,192]{0,1:T(8,128)(2,1)}), bf16[1024,192]{0,1:T(8,128)(2,1)}) %reduce-scatter.20.cloned.1.call-update) | async-done | bytes 393232 | tf_op jit(solution)/shard_map/reduce_scatter | solution.py:36
  836.9 6.6 all-reduce.2
  845.5 35.7 %all-gather.27.cloned.1.call-done = bf16[4096,192]{0,1:T(8,128)(2,1)} async-done(((bf16[1024,192]{0,1:T(8,128)(2,1)}), bf16[4096,192]{0,1:T(8,128)(2,1)}) %all-gather.27.cloned.1.call-update) | async-done | bytes 1572880 | tf_op jit(solution)/shard_map/all_gather | solution.py:32
  885.3 36.6 %reduce-scatter.22.cloned.1.call-done = f32[1024,192]{0,1:T(8,128)} async-done(((f32[4096,192]{0,1:T(8,128)}), f32[1024,192]{0,1:T(8,128)}) %reduce-scatter.22.cloned.1.call-update) | async-done | bytes 786448 | tf_op jit(solution)/shard_map/reduce_scatter | solution.py:46
  923.1 10.9 multiply_reduce_fusion.2
  934.1 12.9 multiply_convert_fusion.2
  952.8 8.8 multiply_reduce_fusion
  961.7 11.2 multiply_convert_fusion
  972.9 10.9 multiply_reduce_fusion.1
  983.8 12.3 multiply_convert_fusion.1
  1005.4 9.5 fusion.19
  1014.9 9.5 fusion.22
  1028.7 6.2 fusion.50
  1035.0 7.9 fusion.49
  1046.6 40.2 %reduce-scatter.24.cloned.1.call-done = f32[1024,384]{0,1:T(8,128)} async-done(((f32[4096,384]{0,1:T(8,128)}), f32[1024,384]{0,1:T(8,128)}) %reduce-scatter.24.cloned.1.call-update) | async-done | bytes 1572880 | tf_op jit(solution)/shard_map/reduce_scatter | solution.py:46
  1089.5 4.7 convolution_convert_fusion.3
  1095.3 6.5 convolution_convert_fusion.4
  1103.1 24.0 %all-gather.29.cloned.1.call-done = bf16[4096,576]{0,1:T(8,128)(2,1)} async-done(((bf16[1024,576]{0,1:T(8,128)(2,1)}), bf16[4096,576]{0,1:T(8,128)(2,1)}) %all-gather.29.cloned.1.call-update) | async-done | bytes 4718608 | tf_op jit(solution)/shard_map/all_gather | solution.py:42
  1143.4 9.8 all_to_all.130
  1153.3 24.1 %all-reduce.10.cloned.1.call-done = (bf16[4,48,192]{2,1,0:T(8,128)(2,1)}, bf16[4,48,192]{2,1,0:T(8,128)(2,1)}, bf16[4,48,192]{2,1,0:T(8,128)(2,1)}, bf16[4,48,19...) async-done(((bf16[4,48,192]{2,1,0:T(8,128)(2,1)}, bf16[4,48,192]{2,1,0:T(8,128)(2,1)}, bf16[4,48,192]{2,1,0:T(8,128)(2,1)}, ...) | async-done | bytes 884752 | tf_op jit(solution)/shard_map/psum | solution.py:263
  1177.4 3.9 all-to-all-start.7
  1193.2 41.5 %all-reduce.1 = (f32[768]{0:T(1024)}, f32[768]{0:T(1024)}, f32[3072]{0:T(1024)}, f32[768]{0:T(1024)}, f32[768]{0:T(1024)}, /*index=5*/f32[768]{0:T(1024)}) all-reduce(f32[768]{0:T(1024)} %dynamic_update_slice.18, f32[768]{0:T(1024)} %dynamic_update_slice.19, ...), channel_id=1, replica_groups=mesh['dp'=2,'row'=4,'col'=4] {'dp','row','col'}, use_global_device_ids=true, to_apply=%region_45.46 | all-reduce | flops 6912 | bytes 55296 | tf_op jit(solution)/shard_map/psum | solution.py:274
  1249.9 5.2 all-reduce.6
  1257.6 5.1 all-to-all-start.6
  1264.5 4.0 all-to-all-done.6
  1271.8 5.8 all-to-all-done.5
  1283.3 5.1 all-to-all-done.8
  (267 shorter events, 137.2 us)
Async XLA Ops:
  7.2 15.4 %copy-start.20 = (f32[48,768]{1,0:T(8,128)S(1)}, f32[48,768]{1,0:T(8,128)}, u32[]{:S(2)}) copy-start(f32[48,768]{1,0:T(8,128)} %param.23) | copy-start | bytes 442372
  7.2 64.8 %all-gather.11.cloned.1.call-start = ((), (), s32[]{:S(2)}) async-start(), calls=%async_computation.18 | async-start | bytes 1966080 | tf_op jit(solution)/shard_map/all_gather | solution.py:32
  20.7 136.6 %reduce-scatter.10.cloned.1.call-start = ((), (), s32[]{:S(2)}) async-start(), calls=%async_computation.19 | async-start | bytes 11796480 | tf_op jit(solution)/shard_map/reduce_scatter | solution.py:46
  78.7 81.9 %copy-start.46 = (f32[192]{0:T(256)S(1)}, f32[192]{0:T(256)}, u32[]{:S(2)}) copy-start(f32[192]{0:T(256)} %param.24) | copy-start | bytes 2308
  78.7 109.8 %all-gather.13.cloned.1.call-start = ((), (), s32[]{:S(2)}) async-start(), calls=%async_computation.20 | async-start | bytes 3932160 | tf_op jit(solution)/shard_map/all_gather | solution.py:42
  159.8 120.3 %all-gather.15.cloned.1.call-start = ((), (), s32[]{:S(2)}) async-start(), calls=%async_computation.21 | async-start | bytes 1966080 | tf_op jit(solution)/shard_map/all_gather | solution.py:42
  196.7 40.9 %copy-start.27 = (f32[1024]{0:T(1024)}, f32[1024]{0:T(1024)S(1)}, u32[]{:S(2)}) copy-start(f32[1024]{0:T(1024)S(1)} %get-tuple-element.101) | copy-start | bytes 12292
  204.8 32.8 %copy-start.37 = (f32[1024]{0:T(1024)}, f32[1024]{0:T(1024)S(1)}, u32[]{:S(2)}) copy-start(f32[1024]{0:T(1024)S(1)} %fusion.2) | copy-start | bytes 12292
  213.0 32.7 %copy-start.29 = (f32[1024]{0:T(1024)}, f32[1024]{0:T(1024)S(1)}, u32[]{:S(2)}) copy-start(f32[1024]{0:T(1024)S(1)} %get-tuple-element.103) | copy-start | bytes 12292
  221.1 24.6 %copy-start.39 = (f32[1024]{0:T(1024)}, f32[1024]{0:T(1024)S(1)}, u32[]{:S(2)}) copy-start(f32[1024]{0:T(1024)S(1)} %fusion.1) | copy-start | bytes 12292
  229.4 22.3 %copy-start.31 = (f32[1024]{0:T(1024)}, f32[1024]{0:T(1024)S(1)}, u32[]{:S(2)}) copy-start(f32[1024]{0:T(1024)S(1)} %get-tuple-element.105) | copy-start | bytes 12292
  229.4 16.4 %slice-start.4 = ((s8[16777216]{0:T(1024)(128)(4,1)}), s8[4194304]{0:T(1024)(128)(4,1)S(1)}, s32[]{:S(2)}) async-start(s8[16777216]{0:T(1024)(128)(4,1)} %bitcast.90), calls=%async_computation.42 | async-start | bytes 8388608
  237.6 14.1 %copy-start.41 = (f32[1024]{0:T(1024)}, f32[1024]{0:T(1024)S(1)}, u32[]{:S(2)}) copy-start(f32[1024]{0:T(1024)S(1)} %fusion) | copy-start | bytes 12292
  237.7 9.6 slice-start.7
  259.5 59.4 %copy-start.3 = (bf16[4,24,8,256]{3,2,0,1:T(8,128)(2,1)S(1)}, bf16[4,24,8,256]{3,2,0,1:T(8,128)(2,1)}, u32[]{:S(2)}) copy-start(bf16[4,24,8,256]{3,2,0,1:T(8,128)(2,1)} %copy.73) | copy-start | bytes 1179652
  259.5 59.4 %copy-start.25 = (f32[192]{0:T(256)S(1)}, f32[192]{0:T(256)}, u32[]{:S(2)}) copy-start(f32[192]{0:T(256)} %param.27) | copy-start | bytes 2308
  260.3 66.4 %copy-start.33 = (f32[192]{0:T(256)S(1)}, f32[192]{0:T(256)}, u32[]{:S(2)}) copy-start(f32[192]{0:T(256)} %param.28) | copy-start | bytes 2308
  260.3 66.4 %copy-start.43 = (f32[192]{0:T(256)S(1)}, f32[192]{0:T(256)}, u32[]{:S(2)}) copy-start(f32[192]{0:T(256)} %param.29) | copy-start | bytes 2308
  260.3 58.5 %reduce-scatter.12.cloned.1.call-start = ((), (), s32[]{:S(2)}) async-start(), calls=%async_computation.22 | async-start | bytes 1966080 | tf_op jit(solution)/shard_map/reduce_scatter | solution.py:36
  266.3 62.4 %copy-start.15 = (bf16[192,768]{1,0:T(8,128)(2,1)}, bf16[192,768]{1,0:T(8,128)(2,1)S(1)}, u32[]{:S(2)}) copy-start(bf16[192,768]{1,0:T(8,128)(2,1)S(1)} %all_gather.48) | copy-start | bytes 884740
  266.3 98.2 %copy-start.16 = (f32[192,768]{1,0:T(8,128)S(1)}, f32[192,768]{1,0:T(8,128)}, u32[]{:S(2)}) copy-start(f32[192,768]{1,0:T(8,128)} %param.30) | copy-start | bytes 1769476
  283.4 81.2 %all-gather.17.cloned.1.call-start = ((), (), s32[]{:S(2)}) async-start(), calls=%async_computation.23 | async-start | bytes 1966080 | tf_op jit(solution)/shard_map/all_gather | solution.py:32
  328.8 141.7 %reduce-scatter.14.cloned.1.call-start = ((), (), s32[]{:S(2)}) async-start(), calls=%async_computation.24 | async-start | bytes 15728640 | tf_op jit(solution)/shard_map/reduce_scatter | solution.py:46
  372.4 98.1 %copy-start.35 = (f32[768]{0:T(1024)S(1)}, f32[768]{0:T(1024)}, u32[]{:S(2)}) copy-start(f32[768]{0:T(1024)} %param.31) | copy-start | bytes 9220
  372.4 117.7 %all-gather.21.cloned.1.call-start = ((), (), s32[]{:S(2)}) async-start(), calls=%async_computation.26 | async-start | bytes 1474560 | tf_op jit(solution)/shard_map/all_gather | solution.py:151
  374.2 163.9 %all-gather.19.cloned.1.call-start = ((), (), s32[]{:S(2)}) async-start(), calls=%async_computation.25 | async-start | bytes 7864320 | tf_op jit(solution)/shard_map/all_gather | solution.py:42
  479.6 64.8 %copy-start.18 = (bf16[256,768]{1,0:T(8,128)(2,1)S(1)}, bf16[256,768]{1,0:T(8,128)(2,1)}, u32[]{:S(2)}) copy-start(bf16[256,768]{1,0:T(8,128)(2,1)} %param.19) | copy-start | bytes 1179652
  479.6 100.2 %reduce-scatter.16.cloned.1.call-start = ((), (), s32[]{:S(2)}) async-start(), calls=%async_computation.27 | async-start | bytes 1966080 | tf_op jit(solution)/shard_map/reduce_scatter | solution.py:36
  544.4 11.8 copy-start.36
  544.4 35.5 %copy-start.4 = (bf16[1024,192]{0,1:T(8,128)(2,1)S(1)}, bf16[1024,192]{0,1:T(8,128)(2,1)}, u32[]{:S(2)}) copy-start(bf16[1024,192]{0,1:T(8,128)(2,1)} %reduce-scatter.12.cloned.1.call-done) | copy-start | bytes 1179652
  544.4 35.5 %copy-start.44 = (f32[192]{0:T(256)S(1)}, f32[192]{0:T(256)}, u32[]{:S(2)}) copy-start(f32[192]{0:T(256)} %param.33) | copy-start | bytes 2308
  545.3 10.9 all-to-all-start.2
  548.8 83.4 %all-gather.23.cloned.1.call-start = ((), (), s32[]{:S(2)}) async-start(), calls=%async_computation.28 | async-start | bytes 1966080 | tf_op jit(solution)/shard_map/all_gather | solution.py:32
  587.9 52.4 %copy-start.22 = (f32[1024]{0:T(1024)}, f32[1024]{0:T(1024)S(1)}, u32[]{:S(2)}) copy-start(f32[1024]{0:T(1024)S(1)} %get-tuple-element.98) | copy-start | bytes 12292
  594.6 45.7 %copy-start.23 = (f32[1024]{0:T(1024)}, f32[1024]{0:T(1024)S(1)}, u32[]{:S(2)}) copy-start(f32[1024]{0:T(1024)S(1)} %get-tuple-element.113) | copy-start | bytes 12292
  594.7 45.7 %copy-start.24 = (f32[1024]{0:T(1024)}, f32[1024]{0:T(1024)S(1)}, u32[]{:S(2)}) copy-start(f32[1024]{0:T(1024)S(1)} %get-tuple-element.114) | copy-start | bytes 12292
  596.3 142.1 %reduce-scatter.18.cloned.1.call-start = ((), (), s32[]{:S(2)}) async-start(), calls=%async_computation.29 | async-start | bytes 15728640 | tf_op jit(solution)/shard_map/reduce_scatter | solution.py:46
  640.4 151.6 %all-gather.25.cloned.1.call-start = ((), (), s32[]{:S(2)}) async-start(), calls=%async_computation.30 | async-start | bytes 7864320 | tf_op jit(solution)/shard_map/all_gather | solution.py:42
  745.5 88.1 %reduce-scatter.20.cloned.1.call-start = ((), (), s32[]{:S(2)}) async-start(), calls=%async_computation.31 | async-start | bytes 1966080 | tf_op jit(solution)/shard_map/reduce_scatter | solution.py:36
  798.1 83.1 %all-gather.27.cloned.1.call-start = ((), (), s32[]{:S(2)}) async-start(), calls=%async_computation.32 | async-start | bytes 1966080 | tf_op jit(solution)/shard_map/all_gather | solution.py:32
  845.4 39.8 %copy-start.28 = (f32[1024]{0:T(1024)S(1)}, f32[1024]{0:T(1024)}, u32[]{:S(2)}) copy-start(f32[1024]{0:T(1024)} %copy-done.27) | copy-start | bytes 12292
  845.4 39.8 %copy-start.38 = (f32[1024]{0:T(1024)S(1)}, f32[1024]{0:T(1024)}, u32[]{:S(2)}) copy-start(f32[1024]{0:T(1024)} %copy-done.37) | copy-start | bytes 12292
  845.4 39.8 %copy-start.30 = (f32[1024]{0:T(1024)S(1)}, f32[1024]{0:T(1024)}, u32[]{:S(2)}) copy-start(f32[1024]{0:T(1024)} %copy-done.29) | copy-start | bytes 12292
  845.4 39.8 %copy-start.40 = (f32[1024]{0:T(1024)S(1)}, f32[1024]{0:T(1024)}, u32[]{:S(2)}) copy-start(f32[1024]{0:T(1024)} %copy-done.39) | copy-start | bytes 12292
  845.4 39.8 %copy-start.32 = (f32[1024]{0:T(1024)S(1)}, f32[1024]{0:T(1024)}, u32[]{:S(2)}) copy-start(f32[1024]{0:T(1024)} %copy-done.31) | copy-start | bytes 12292
  845.4 39.8 %copy-start.42 = (f32[1024]{0:T(1024)S(1)}, f32[1024]{0:T(1024)}, u32[]{:S(2)}) copy-start(f32[1024]{0:T(1024)} %copy-done.41) | copy-start | bytes 12292
  845.4 76.5 %reduce-scatter.22.cloned.1.call-start = ((), (), s32[]{:S(2)}) async-start(), calls=%async_computation.33 | async-start | bytes 3932160 | tf_op jit(solution)/shard_map/reduce_scatter | solution.py:46
  885.0 201.8 %reduce-scatter.24.cloned.1.call-start = ((), (), s32[]{:S(2)}) async-start(), calls=%async_computation.34 | async-start | bytes 7864320 | tf_op jit(solution)/shard_map/reduce_scatter | solution.py:46
  934.1 18.7 %slice-start = ((s8[16777216]{0:T(1024)(128)(4,1)}), s8[4194304]{0:T(1024)(128)(4,1)S(1)}, s32[]{:S(2)}) async-start(s8[16777216]{0:T(1024)(128)(4,1)} %bitcast.88), calls=%async_computation.38 | async-start | bytes 8388608
  934.1 18.7 %slice-start.1 = ((s8[16777216]{0:T(1024)(128)(4,1)}), s8[4194304]{0:T(1024)(128)(4,1)S(1)}, s32[]{:S(2)}) async-start(s8[16777216]{0:T(1024)(128)(4,1)} %bitcast.88), calls=%async_computation.39 | async-start | bytes 8388608
  934.1 18.7 %slice-start.2 = ((s8[16777216]{0:T(1024)(128)(4,1)}), s8[4194304]{0:T(1024)(128)(4,1)S(1)}, s32[]{:S(2)}) async-start(s8[16777216]{0:T(1024)(128)(4,1)} %bitcast.88), calls=%async_computation.40 | async-start | bytes 8388608
  1028.3 98.8 %all-gather.29.cloned.1.call-start = ((), (), s32[]{:S(2)}) async-start(), calls=%async_computation.35 | async-start | bytes 5898240 | tf_op jit(solution)/shard_map/all_gather | solution.py:42
  1028.7 14.2 %slice-start.8 = ((s8[8388608]{0:T(1024)(128)(4,1)}), s8[4194304]{0:T(1024)(128)(4,1)S(1)}, s32[]{:S(2)}) async-start(s8[8388608]{0:T(1024)(128)(4,1)} %bitcast.92), calls=%async_computation.46 | async-start | bytes 8388608
  1089.4 88.0 %all-reduce.10.cloned.1.call-start = ((), (), s32[]{:S(2)}) async-start(), calls=%async_computation.37 | async-start | bytes 2162688 | tf_op jit(solution)/shard_map/psum | solution.py:263
  1135.6 145.5 %reduce-scatter.26.cloned.1.call-start = ((), (), s32[]{:S(2)}) async-start(), calls=%async_computation.36 | async-start | bytes 1966080 | tf_op jit(solution)/shard_map/reduce_scatter | solution.py:36
  1177.4 66.5 %all-to-all-start.7 = ((bf16[4,48,192]{2,1,0:T(8,128)(2,1)}), bf16[4,48,192]{2,1,0:T(8,128)(2,1)}, u32[]{:S(2)}, u32[]{:S(2)}) async-start(bf16[4,48,192]{2,1,0:T(8,128)(2,1)} %get-tuple-element.85), calls=%async_computation.16 | async-start | bytes 196608 | tf_op jit(solution)/shard_map/all_to_all | solution.py:303
  1243.6 13.1 %copy-start.19 = (bf16[192,768]{1,0:T(8,128)(2,1)S(1)}, bf16[192,768]{1,0:T(8,128)(2,1)}, u32[]{:S(2)}) copy-start(bf16[192,768]{1,0:T(8,128)(2,1)} %get-tuple-element.86) | copy-start | bytes 884740
  1243.9 13.7 %all-to-all-start.4 = ((bf16[4,48,192]{2,1,0:T(8,128)(2,1)}), bf16[4,48,192]{2,1,0:T(8,128)(2,1)S(1)}, u32[]{:S(2)}, u32[]{:S(2)}) async-start(bf16[4,48,192]{2,1,0:T(8,128)(2,1)} %get-tuple-element.82), calls=%async_computation.13 | async-start | bytes 196608 | tf_op jit(solution)/shard_map/all_to_all | solution.py:292
  1247.5 33.7 %copy-start.26 = (f32[192]{0:T(256)S(1)}, f32[192]{0:T(256)}, u32[]{:S(2)}) copy-start(f32[192]{0:T(256)} %param.27) | copy-start | bytes 2308
  1247.5 33.7 %copy-start.34 = (f32[192]{0:T(256)S(1)}, f32[192]{0:T(256)}, u32[]{:S(2)}) copy-start(f32[192]{0:T(256)} %param.28) | copy-start | bytes 2308
  1257.6 10.9 all-to-all-start.6
  1268.5 9.1 all-to-all-start.5
  1277.6 10.9 all-to-all-start.8
  1288.5 10.9 all-to-all-start.3
  (20 other events, 99.6 us)
Sparse Core Ops, SparseCore 0:
  20.8 47.8 all-gather.10
  78.9 78.4 reduce-scatter.9
  159.9 28.5 all-gather.12
  260.4 19.6 all-gather.14
  283.5 35.2 reduce-scatter.11
  328.9 35.6 all-gather.16
  372.5 97.9 reduce-scatter.13
  472.6 17.4 all-gather.20
  491.7 46.3 all-gather.18
  544.5 35.2 reduce-scatter.15
  596.4 35.7 all-gather.22
  640.5 97.9 reduce-scatter.17
  745.6 46.3 all-gather.24
  798.3 35.2 reduce-scatter.19
  845.5 35.6 all-gather.26
  885.1 36.7 reduce-scatter.21
  1028.4 58.3 reduce-scatter.23
  1089.6 37.4 all-gather.28
  1135.7 41.6 all-reduce.9
  1179.6 35.4 reduce-scatter.25
where the time goes:
time: 1310 us
  waiting for transfers between devices  769 us (59%)
  matrix products  194 us (15%)
  blocking collectives  148 us (11%)
  other arithmetic  109 us (8%)
  local copies, waits for them, and re-layouts  42.7 us (3%)
  starting transfers between devices  28.4 us (2%)
  between operations  16.2 us (1%)
    reduce_scatter x5, waiting for transfers between devices, row_reduce(): return lax.psum_scatter(shard_in, 'row', scatter_dimension=0, tiled=True)  349 us
    all_gather x5, waiting for transfers between devices, row_gather(): return lax.all_gather(shard_in, 'row', axis=0, tiled=True)  159 us
    all_gather x4, waiting for transfers between devices, across_cols(): return lax.all_gather(shard_in, 'col', axis=0, tiled=True)  107 us
    reduce_scatter x4, waiting for transfers between devices, col_sums(): lax.psum_scatter(shard_in.astype(jnp.bfloat16), 'col', scatter_dimension=...  93.5 us
    dot_general x12, matrix products, matmul_nt(): lax.dot_general(left_mat, right_mat, (((1,), (1,)), ((), ())), preferred_...  80.8 us
    dot_general x10, matrix products, matmul(): return jnp.dot(left_mat, right_mat, preferred_element_type=jnp.float32)  62.1 us
    dot_general x12, matrix products, matmul_tn(): lax.dot_general(left_mat, right_mat, (((0,), (0,)), ((), ())), preferred_...  51.4 us
    psum x1, blocking collectives, per_device(): lax.psum((place_block(grad_norm1_gain, full_width, row_index), place_bloc...  41.5 us
  transfers between devices with their start and end apart: 27, of which 23 were waited for; matrix products, arithmetic and copies ran while one was open for 7% of the time, Pallas kernels for 0%

commit v1 on v0

v1 whole, which is shorter than its diff:
```python
import functools
import math

import jax
import jax.numpy as jnp
from jax import lax
from jax.experimental import pallas as pl
from jax.experimental.pallas import tpu as pltpu
from jax.sharding import PartitionSpec as P

HD = 64
LANES = 256
EPS = 1e-05
BF = jnp.bfloat16
F32 = jnp.float32
VMEM_BYTES = 60 * 1024 * 1024


def nn(a, b):
    return jnp.dot(a, b, preferred_element_type=F32)


def tn(a, b):
    return lax.dot_general(a, b, (((0,), (0,)), ((), ())), preferred_element_type=F32)


def nt(a, b):
    return lax.dot_general(a, b, (((1,), (1,)), ((), ())), preferred_element_type=F32)


CORE = [(0, 1), (1, 0), (2, 3), (3, 2)]
CROSS = [(0, 2), (2, 0), (1, 3), (3, 1)]


def core_swap(x):
    return lax.ppermute(x, "row", CORE)


def cross_swap(x):
    return lax.ppermute(x, "row", CROSS)


def shift_col(x, step):
    n = lax.axis_size("col")
    return lax.ppermute(x, "col", [(i, (i + step) % n) for i in range(n)])


def gather_row_rel(x):
    near = core_swap(x)
    far = cross_swap(x)
    return [x, near, far, core_swap(far)]


def natural_row(blocks):
    r = lax.axis_index("row")
    low = (r & 1) == 0
    b0, b1, b2, b3 = blocks
    left = jnp.where(low, jnp.concatenate([b0, b1]), jnp.concatenate([b1, b0]))
    right = jnp.where(low, jnp.concatenate([b2, b3]), jnp.concatenate([b3, b2]))
    return jnp.where(r < 2, jnp.concatenate([left, right]), jnp.concatenate([right, left]))


def reduce_row_rel(own, near, far, diag):
    got = core_swap(jnp.stack([near, diag]).astype(BF))
    own = own + got[0].astype(F32)
    far = far + got[1].astype(F32)
    return own + cross_swap(far.astype(BF)).astype(F32)


def gather_col(x):
    n = lax.axis_size("col")
    z = lax.axis_index("col")
    out = jnp.zeros((n,) + x.shape, x.dtype)
    block = x
    out = lax.dynamic_update_index_in_dim(out, block, z, 0)
    for step in range(1, n):
        block = shift_col(block, 1)
        out = lax.dynamic_update_index_in_dim(out, block, (z + n - step) % n, 0)
    return out


def reduce_col(parts):
    n = lax.axis_size("col")
    z = lax.axis_index("col")

    def part(k):
        return lax.dynamic_index_in_dim(parts, (z + n - k) % n, 0, keepdims=False)

    total = part(1)
    for step in range(2, n + 1):
        total = part(step) + shift_col(total.astype(BF), 1).astype(F32)
    return total


def sum_dp(x):
    n = lax.axis_size("dp")
    if n == 2:
        return x + lax.ppermute(x, "dp", [(0, 1), (1, 0)])
    return lax.psum(x, "dp")


def split3(x):
    hi = lax.reduce_precision(x, 8, 7)
    mid = lax.reduce_precision(x - hi, 8, 7)
    low = x - hi - mid
    return hi.astype(BF), mid.astype(BF), low.astype(BF)


def head_lanes(shape, head, width):
    lane = lax.broadcasted_iota(jnp.int32, shape, 1)
    mine = (lane >= head * HD) & (lane < (head + 1) * HD)
    return mine | (lane == width) | ((lane >= width + 1 + 3 * head) & (lane < width + 4 + 3 * head))


def attn_fwd_kernel(q_ref, k_ref, v_ref, o_ref, lse_ref, *, heads, chunk):
    width = heads * HD
    q = q_ref[...]
    out = jnp.zeros(o_ref.shape, F32)
    lse = jnp.zeros(lse_ref.shape, F32)
    lane = lax.broadcasted_iota(jnp.int32, lse_ref.shape, 1)
    for head in range(heads):
        mine = head_lanes(q.shape, head, width)
        qh = jnp.where(mine, q, jnp.zeros_like(q))
        acc = None
        for j in range(k_ref.shape[0] // chunk):
            rows = slice(j * chunk, (j + 1) * chunk)
            s = nt(qh, k_ref[rows, :])
            top = jnp.max(s, axis=1, keepdims=True)
            if acc is None:
                peak = top
                acc = nn(jnp.exp(s - peak).astype(BF), v_ref[rows, :])
            else:
                new = jnp.maximum(peak, top)
                acc = acc * jnp.exp(peak - new) + nn(jnp.exp(s - new).astype(BF), v_ref[rows, :])
                peak = new
        total = acc[:, width : width + 1]
        out = jnp.where(mine, acc / total, out)
        lse = jnp.where(lane == head, peak + jnp.log(total), lse)
    o_ref[...] = out.astype(o_ref.dtype)
    lse_ref[...] = lse


def attn_fwd(q, k, v, heads, block=256, chunk=2048):
    rows = q.shape[0]
    keys = k.shape[0]
    whole = pl.BlockSpec((keys, LANES), lambda i: (0, 0))
    return pl.pallas_call(
        functools.partial(attn_fwd_kernel, heads=heads, chunk=min(chunk, keys)),
        grid=(rows // block,),
        in_specs=[pl.BlockSpec((block, LANES), lambda i: (i, 0)), whole, whole],
        out_specs=[
            pl.BlockSpec((block, LANES), lambda i: (i, 0)),
            pl.BlockSpec((block, 128), lambda i: (i, 0)),
        ],
        out_shape=[
            jax.ShapeDtypeStruct((rows, LANES), BF),
            jax.ShapeDtypeStruct((rows, 128), F32),
        ],
        compiler_params=pltpu.CompilerParams(vmem_limit_bytes=VMEM_BYTES),
        cost_estimate=pl.CostEstimate(
            flops=4 * rows * keys * LANES * heads,
            bytes_accessed=4 * (rows + keys) * LANES,
            transcendentals=heads * rows * keys,
        ),
        name="attn_fwd",
    )(q, k, v)


def attn_bwd_kernel(q_ref, do_ref, k_ref, v_ref, dq_ref, dk_ref, dv_ref, dq_acc, *, heads, block):
    width = heads * HD
    step = pl.program_id(0)
    k = k_ref[...]
    v = v_ref[...]

    @pl.when(step == 0)
    def _():
        dq_acc[...] = jnp.zeros_like(dq_acc)

    dk = jnp.zeros(dk_ref.shape, F32)
    dv = jnp.zeros(dv_ref.shape, F32)
    for i in range(q_ref.shape[0] // block):
        rows = slice(i * block, (i + 1) * block)
        q_all = q_ref[rows, :]
        do_all = do_ref[rows, :]
        dq = jnp.zeros((block, LANES), F32)
        for head in range(heads):
            mine = head_lanes((block, LANES), head, width)
            q = jnp.where(mine, q_all, jnp.zeros_like(q_all))
            do = jnp.where(mine, do_all, jnp.zeros_like(do_all))
            p = jnp.exp(nt(k, q))
            ds = (p * nt(v, do)).astype(BF)
            dv = dv + nn(p.astype(BF), do)
            dk = dk + nn(ds, q)
            dq = jnp.where(mine, tn(ds, k), dq)
        dq_acc[rows, :] += dq
    dk_ref[...] = dk.astype(dk_ref.dtype)
    dv_ref[...] = dv.astype(dv_ref.dtype)

    @pl.when(step == pl.num_programs(0) - 1)
    def _():
        dq_ref[...] = dq_acc[...].astype(dq_ref.dtype)


def attn_bwd(q, do, k, v, heads, block=256, chunk=1024):
    rows = q.shape[0]
    keys = k.shape[0]
    whole = pl.BlockSpec((rows, LANES), lambda i: (0, 0))
    part = pl.BlockSpec((chunk, LANES), lambda i: (i, 0))
    return pl.pallas_call(
        functools.partial(attn_bwd_kernel, heads=heads, block=block),
        grid=(keys // chunk,),
        in_specs=[whole, whole, part, part],
        out_specs=[whole, part, part],
        out_shape=[
            jax.ShapeDtypeStruct((rows, LANES), F32),
            jax.ShapeDtypeStruct((keys, LANES), F32),
            jax.ShapeDtypeStruct((keys, LANES), F32),
        ],
        scratch_shapes=[pltpu.VMEM((rows, LANES), F32)],
        compiler_params=pltpu.CompilerParams(vmem_limit_bytes=VMEM_BYTES),
        cost_estimate=pl.CostEstimate(
            flops=10 * rows * keys * LANES * heads,
            bytes_accessed=8 * (rows + keys) * LANES,
            transcendentals=heads * rows * keys,
        ),
        name="attn_bwd",
    )(q, do, k, v)


def gelu_exact(x):
    return jax.nn.gelu(x, approximate=False)


def norm_forward(resid, gain, shift):
    mean = jnp.mean(resid, axis=1, keepdims=True)
    centered = resid - mean
    inv = lax.rsqrt(jnp.mean(centered * centered, axis=1, keepdims=True) + EPS)
    normal = centered * inv
    return normal * gain + shift, normal, inv


def norm_backward(grad_out, normal, inv, gain):
    scaled = grad_out * gain
    mean_e = jnp.mean(scaled, axis=1, keepdims=True)
    mean_en = jnp.mean(scaled * normal, axis=1, keepdims=True)
    grad_in = inv * (scaled - mean_e - normal * mean_en)
    return grad_in, jnp.sum(grad_out * normal, axis=0), jnp.sum(grad_out, axis=0)


def per_device(
    tokens,
    cotangent,
    lengths,
    query_weight,
    key_weight,
    value_weight,
    query_bias,
    value_bias,
    out_weight,
    out_bias,
    norm1_gain,
    norm1_shift,
    up_weight,
    up_bias,
    down_weight,
    down_bias,
    norm2_gain,
    norm2_shift,
):
    rows_n = lax.axis_size("row")
    cols_n = lax.axis_size("col")
    r = lax.axis_index("row")
    z = lax.axis_index("col")
    local, width = tokens.shape
    block_len = local * cols_n
    length = lengths[0]
    hw = width // cols_n
    heads = hw // HD
    feat = width // rows_n
    scale = 1.0 / math.sqrt(HD)

    x_col = gather_col(tokens).reshape(block_len, width)

    qkv = jnp.stack([query_weight, key_weight, value_weight], axis=1).astype(BF)
    sub = qkv.shape[0]
    qkv = qkv.reshape(sub, 3, cols_n, hw).transpose(2, 0, 1, 3).reshape(cols_n, sub, 3 * hw)
    qkv = lax.all_to_all(qkv, "col", split_axis=0, concat_axis=0, tiled=True)
    qkv = qkv.reshape(cols_n * sub, 3 * hw)
    vecs = jnp.stack([out_bias, norm1_gain, norm1_shift, down_bias, norm2_gain, norm2_shift])
    vec_parts = jnp.stack(split3(vecs)).reshape(-1)
    vec_rows = 16
    vec_parts = jnp.pad(vec_parts, (0, vec_rows * 3 * hw - vec_parts.shape[0]))
    message = jnp.concatenate([qkv, vec_parts.reshape(vec_rows, 3 * hw)])
    got = natural_row([b[None] for b in gather_row_rel(message)])
    w_qkv = got[:, : cols_n * sub].reshape(width, 3 * hw)
    vec_all = got[:, cols_n * sub :].reshape(rows_n, -1)[:, : 3 * 6 * feat]
    vec_all = jnp.sum(vec_all.reshape(rows_n, 3, 6, feat).astype(F32), axis=1)
    vec_all = vec_all.transpose(1, 0, 2).reshape(6, width)
    out_bias_all, gain1, shift1, down_bias_all, gain2, shift2 = [vec_all[i] for i in range(6)]

    up_t = up_weight.astype(BF).T
    units = up_t.shape[0] // rows_n
    up_t = up_t.reshape(rows_n, units, feat)
    up_t = lax.all_to_all(up_t, "row", split_axis=0, concat_axis=0, tiled=True)
    up_t = up_t.transpose(1, 0, 2).reshape(units, width)
    bias_mine = lax.dynamic_slice_in_dim(up_bias, r * units, units, 0)
    bias_rows = jnp.pad(jnp.stack(split3(bias_mine)), ((0, 13), (0, width - units)))
    sub_out = out_weight.shape[0]
    pack = jnp.concatenate([up_t, down_weight.astype(BF), out_weight.astype(BF), bias_rows])
    pack = lax.all_gather(pack, "col", axis=0, tiled=False)
    up_r = pack[:, :units].reshape(cols_n * units, width)
    down_r = pack[:, units : 2 * units].reshape(cols_n * units, width)
    out_r = pack[:, 2 * units : 2 * units + sub_out]
    up_bias_r = jnp.sum(pack[:, 2 * units + sub_out :][:, :3, :units].astype(F32), axis=1)
    up_bias_r = up_bias_r.reshape(1, cols_n * units)

    proj = nn(x_col, w_qkv)
    proj_bias = jnp.concatenate([query_bias, jnp.zeros_like(query_bias), value_bias])
    proj = (proj + proj_bias).astype(BF)
    queries = proj[:, :hw]
    kv = jnp.concatenate(gather_row_rel(proj[:, hw:]))
    keys_n = kv.shape[0]
    place = jnp.arange(keys_n, dtype=jnp.int32)
    owner = r ^ (place // block_len)
    inner = place % block_len
    position = (inner // local) * (local * rows_n) + owner * local + inner % local
    key_mask = jnp.where(position < length, 0.0, -1e30).astype(BF)[:, None]
    pad_n = LANES - hw - 1
    key_rows = jnp.concatenate([kv[:, :hw], key_mask, jnp.ones((keys_n, pad_n), BF)], axis=1)
    value_rows = jnp.concatenate([kv[:, hw:], jnp.ones((keys_n, pad_n + 1), BF)], axis=1)
    q_scaled = queries * jnp.asarray(scale, BF)
    ones_q = jnp.ones((block_len, 1), BF)
    q_rows = jnp.concatenate([q_scaled, ones_q, jnp.zeros((block_len, pad_n), BF)], axis=1)
    mixed_wide, lse = attn_fwd(q_rows, key_rows, value_rows, heads)
    mixed_part = mixed_wide[:, :hw]
    mixed = lax.all_to_all(mixed_part, "col", split_axis=0, concat_axis=1, tiled=True)

    out_full = natural_row([b[None] for b in gather_row_rel(out_r)])
    out_full = out_full.transpose(1, 0, 2, 3).reshape(width, width)
    attended = nn(mixed, out_full) + out_bias_all
    hidden, normal1, inv1 = norm_forward(tokens.astype(F32) + attended, gain1, shift1)

    hidden_all = jnp.concatenate(gather_row_rel(hidden.astype(BF)))
    preact = nt(hidden_all, up_r) + up_bias_r
    active = gelu_exact(preact).astype(BF)
    part = nn(active, down_r).reshape(rows_n, local, width)
    branch = reduce_row_rel(part[0], part[1], part[2], part[3]) + down_bias_all
    normed, normal2, inv2 = norm_forward(hidden + branch, gain2, shift2)
    my_pos = z * (local * rows_n) + r * local + jnp.arange(local, dtype=jnp.int32)
    valid = (my_pos < length).astype(F32)[:, None]
    output = (normed * valid).astype(BF)

    grad_y = cotangent.astype(F32) * valid
    grad_resid2, g_gain2, g_shift2 = norm_backward(grad_y, normal2, inv2, gain2)
    grad_branch = grad_resid2.astype(BF)
    g_down_bias = jnp.sum(grad_branch.astype(F32), axis=0)
    grad_branch_all = jnp.concatenate(gather_row_rel(grad_branch))
    grad_active = nt(grad_branch_all, down_r)
    grad_preact = jax.vjp(gelu_exact, preact)[1](grad_active)[0].astype(BF)
    part = nn(grad_preact, up_r).reshape(rows_n, local, width)
    grad_hidden = reduce_row_rel(part[0], part[1], part[2], part[3]) + grad_resid2
    g_down = tn(active, grad_branch_all).astype(BF).reshape(cols_n, units, width)
    g_up = tn(grad_preact, hidden_all).astype(BF).reshape(cols_n, units, width)
    g_up_bias = jnp.sum(grad_preact.astype(F32), axis=0)
    grad_resid1, g_gain1, g_shift1 = norm_backward(grad_hidden, normal1, inv1, gain1)
    grad_attended = grad_resid1.astype(BF)
    g_out_bias = jnp.sum(grad_attended.astype(F32), axis=0)
    grad_mixed_local = nt(grad_attended, out_full).astype(BF)
    grad_mixed = lax.all_to_all(grad_mixed_local, "col", split_axis=1, concat_axis=0, tiled=True)

    g_out = tn(mixed, grad_attended).reshape(cols_n, rows_n, sub_out, width)
    g_out = [lax.dynamic_index_in_dim(g_out, r ^ k, 1, keepdims=False) for k in range(4)]
    g_out = reduce_row_rel(*g_out).astype(BF)
    g_pack = jnp.concatenate([g_up, g_down, g_out], axis=1)
    g_pack = lax.psum_scatter(g_pack, "col", scatter_dimension=0, tiled=True)[0]
    g_pack = sum_dp(g_pack)
    g_up = g_pack[:units].reshape(units, rows_n, feat)
    g_up = lax.all_to_all(g_up, "row", split_axis=1, concat_axis=0, tiled=True)
    g_up_weight = g_up.reshape(rows_n * units, feat).T.astype(F32)
    g_down_weight = g_pack[units : 2 * units].astype(F32)
    g_out_weight = g_pack[2 * units :].astype(F32)

    lse_parts = jnp.stack(split3(-lse[:, :heads]), axis=2).reshape(block_len, 3 * heads)
    tail = jnp.zeros((block_len, pad_n - 3 * heads), BF)
    qb_rows = jnp.concatenate([q_scaled, ones_q, lse_parts, tail], axis=1)
    delta = mixed_part.astype(F32) * grad_mixed.astype(F32)
    delta = -jnp.sum(delta.reshape(block_len, heads, HD), axis=2)
    delta_parts = jnp.stack(split3(delta), axis=2).reshape(block_len, 3 * heads)
    do_rows = jnp.concatenate(
        [grad_mixed, jnp.zeros((block_len, 1), BF), delta_parts, tail], axis=1
    )
    dq, dk, dv = attn_bwd(qb_rows, do_rows, key_rows, value_rows, heads)
    grad_q = (dq[:, :hw] * scale).astype(BF)
    grad_kv = jnp.concatenate([dk[:, :hw], dv[:, :hw]], axis=1)
    grad_kv = grad_kv.reshape(rows_n, block_len, 2 * hw)
    grad_kv = reduce_row_rel(*[grad_kv[i] for i in range(4)]).astype(BF)
    grad_qkv = jnp.concatenate([grad_q, grad_kv], axis=1)

    back = nt(grad_qkv, w_qkv).reshape(cols_n, local, width)
    grad_tokens = grad_resid1 + reduce_col(back)

    g_qkv = tn(x_col, grad_qkv).reshape(rows_n, feat, 3 * hw)
    g_bias = jnp.sum(grad_qkv.astype(F32), axis=0)
    g_qkv = [lax.dynamic_index_in_dim(g_qkv, r ^ k, 0, keepdims=False) for k in range(4)]
    g_qkv = sum_dp(reduce_row_rel(*g_qkv).astype(BF))
    g_qkv = lax.all_to_all(
        g_qkv.reshape(cols_n, sub, 3 * hw), "col", split_axis=0, concat_axis=0, tiled=True
    )
    g_qkv = g_qkv.reshape(cols_n, sub, 3, hw).transpose(2, 1, 0, 3).reshape(3, sub, width)
    g_qkv = g_qkv.astype(F32)

    up_place = jnp.zeros((cols_n, rows_n, units), F32)
    up_place = lax.dynamic_update_slice(
        up_place, g_up_bias.reshape(cols_n, 1, units), (0, r, 0)
    ).reshape(-1, width)
    bias_place = jnp.zeros((2, width), F32)
    bias_place = lax.dynamic_update_slice(
        bias_place, jnp.stack([g_bias[:hw], g_bias[2 * hw :]]), (0, z * hw)
    )
    sums = jnp.concatenate(
        [jnp.stack([g_gain1, g_shift1, g_gain2, g_shift2, g_down_bias, g_out_bias]), up_place, bias_place]
    )
    sums = sums + core_swap(sums)
    sums = sums + cross_swap(sums)
    sums = sum_dp(sums)
    sums = sums + lax.ppermute(sums, "col", [(i, i ^ 1) for i in range(cols_n)])
    sums = sums + lax.ppermute(sums, "col", [(i, i ^ 2) for i in range(cols_n)])
    mine = lax.dynamic_slice_in_dim(sums[:6], r * feat, feat, 1)
    g_up_bias = lax.dynamic_index_in_dim(
        sums[6:-2].reshape(cols_n, rows_n * units), z, 0, keepdims=False
    )
    g_bias = lax.dynamic_slice_in_dim(sums[-2:], z * hw, hw, 1)
    return (
        output,
        grad_tokens,
        g_qkv[0],
        g_qkv[1],
        g_qkv[2],
        g_bias[0],
        g_bias[1],
        g_out_weight,
        mine[5],
        mine[0],
        mine[1],
        g_up_weight,
        g_up_bias,
        g_down_weight,
        mine[4],
        mine[2],
        mine[3],
    )


def solution(mesh):
    token_spec = P(("dp", "col", "row"), None)
    placed = (
        token_spec,
        token_spec,
        P("dp"),
        P(("row", "col"), None),
        P(("row", "col"), None),
        P(("row", "col"), None),
        P("col"),
        P("col"),
        P(("col", "row"), None),
        P("row"),
        P("row"),
        P("row"),
        P("row", "col"),
        P("col"),
        P(("col", "row"), None),
        P("row"),
        P("row"),
        P("row"),
    )
    return jax.shard_map(
        per_device,
        mesh=mesh,
        in_specs=placed,
        out_specs=(token_spec, token_spec) + placed[3:],
        check_vma=False,
    )
```

time: 1310 us -> 483 us (0.37)
  waiting for transfers between devices: 769 us -> 191 us
  matrix products: 194 us -> 36.4 us
  blocking collectives: 148 us -> 0 us
  Pallas kernels: 0 us -> 57.1 us
  other arithmetic: 109 us -> 71.4 us
  starting transfers between devices: 28.4 us -> 53.2 us
    reduce_scatter x9 -> x1, waiting for transfers between devices: 442 us -> 0.02 us  [per_device(): g_pack = lax.psum_scatter(g_pack, 'col', scatter_dimension=0, tiled=True)[0]]
    all_gather x10 -> x1, waiting for transfers between devices: 276 us -> 22 us  [per_device(): pack = lax.all_gather(pack, 'col', axis=0, tiled=False)]
    dot_general x34 -> x12, matrix products: 194 us -> 36.4 us  [the longest x4 19.7 us: nt(): lax.dot_general(a, b, (((1,), (1,)), ((), ())), preferred_element_type=F32)]
    ppermute x0 -> x38, waiting for transfers between devices: none -> 142 us  [the longest x11 78.2 us: cross_swap(): return lax.ppermute(x, 'row', CROSS)]
    psum x6 -> x0, blocking collectives: 72.2 us -> none  [the longest x1 41.5 us: per_device(): lax.psum((place_block(grad_norm1_gain, full_width, row_index), place_bloc...]
    pallas_call x0 -> x2, Pallas kernels: none -> 57.1 us  [the longest x1 37.6 us: attn_bwd(): pl.pallas_call(functools.partial(attn_bwd_kernel, heads=heads, block=bloc...]
    all_gather x4 -> x0, blocking collectives: 55 us -> none  [the longest x1 17.3 us: per_device(): lax.all_gather(key_weight.astype(jnp.bfloat16), 'col', axis=0, tiled=True)]
    convert_element_type x28 -> x23, other arithmetic: 63.5 us -> 18.3 us  [the longest x5 6.18 us: reduce_row_rel(): return own + cross_swap(far.astype(BF)).astype(F32)]
  transfers between devices with their start and end apart: 27 -> 46, of which waited for: 23 -> 25; matrix products, arithmetic and copies ran while one was open for 7% -> 23% of each run, Pallas kernels for 0% -> 12%
where the time goes in v1:
time: 483 us; the launch traced here: 475 us
  waiting for transfers between devices  191 us (40%)
  other arithmetic  71.4 us (15%)
  Pallas kernels  57.1 us (12%)
  starting transfers between devices  53.2 us (11%)
  local copies, waits for them, and re-layouts  48.7 us (10%)
  matrix products  36.4 us (8%)
  between operations  16.5 us (3%)
    ppermute x11, waiting for transfers between devices, cross_swap(): return lax.ppermute(x, 'row', CROSS)  78.2 us
    ppermute x6, waiting for transfers between devices, shift_col(): return lax.ppermute(x, 'col', [(i, (i + step) % n) for i in range(n)])  44.6 us
    pallas_call x1, Pallas kernels, attn_bwd(): pl.pallas_call(functools.partial(attn_bwd_kernel, heads=heads, block=bloc...  37.6 us
    all_gather x1, waiting for transfers between devices, per_device(): pack = lax.all_gather(pack, 'col', axis=0, tiled=False)  22 us
    dot_general x4, matrix products, nt(): lax.dot_general(a, b, (((1,), (1,)), ((), ())), preferred_element_type=F32)  19.7 us
    pallas_call x1, Pallas kernels, attn_fwd(): pl.pallas_call(functools.partial(attn_fwd_kernel, heads=heads, chunk=min(...  19.5 us
    ppermute x11, starting transfers between devices, cross_swap(): return lax.ppermute(x, 'row', CROSS)  11 us
    all_to_all x1, waiting for transfers between devices, per_device(): lax.all_to_all(mixed_part, 'col', split_axis=0, concat_axis=1, tiled=True)  10.4 us
  transfers between devices with their start and end apart: 46, of which 25 were waited for; matrix products, arithmetic and copies ran while one was open for 23% of the time, Pallas kernels for 12%

profile of v1, /device:TPU:0, one launch (start us, length us, event | category | flops | bytes accessed | tf_op | source)
XLA Modules:
  0.0 474.8 jit_solution(6416055537266069844)
XLA Ops:
  12.9 6.3 %all-to-all-start = ((bf16[4,48,576]{2,1,0:T(8,128)(2,1)}), bf16[4,48,576]{2,1,0:T(8,128)(2,1)S(1)}, u32[]{:S(2)}, u32[]{:S(2)}) async-start(bf16[4,48,576]{2,1,0:T(8,128)(2,1)} %reshape.736), calls=%async_computation | async-start | bytes 491520 | tf_op jit(solution)/shard_map/all_to_all | solution.py:287
  19.2 2.0 collective-permute-start
  24.9 10.8 %collective-permute-done = bf16[256,768]{1,0:T(8,128)(2,1)S(1)} collective-permute-done((bf16[256,768]{1,0:T(8,128)(2,1)S(1)}, bf16[256,768]{1,0:T(8,128)(2,1)S(1)}, u32[]{:S(2)}, u32[]{:S(2)}) %collective-permute-start) | collective-permute-done | bytes 393248 | tf_op jit(solution)/shard_map/ppermute | solution.py:45
  36.2 4.1 all-to-all-start.2
  40.9 1.7 collective-permute-start.4
  42.6 10.8 %collective-permute-done.4 = bf16[208,576]{1,0:T(8,128)(2,1)S(1)} collective-permute-done((bf16[208,576]{1,0:T(8,128)(2,1)S(1)}, bf16[208,576]{1,0:T(8,128)(2,1)S(1)}, u32[]{:S(2)}, u32[]{:S(2)}) %collective-permute-start.4) | collective-permute-done | bytes 239648 | tf_op jit(solution)/shard_map/ppermute | solution.py:40
  56.3 10.8 %collective-permute-done.2 = bf16[256,768]{1,0:T(8,128)(2,1)S(1)} collective-permute-done((bf16[256,768]{1,0:T(8,128)(2,1)}, bf16[256,768]{1,0:T(8,128)(2,1)S(1)}, u32[]{:S(2)}, u32[]{:S(2)}) %collective-permute-start.2) | collective-permute-done | bytes 393248 | tf_op jit(solution)/shard_map/ppermute | solution.py:45
  71.7 1.9 pad_maximum_fusion.9
  76.5 12.5 %collective-permute-done.7 = bf16[1024,384]{1,0:T(8,128)(2,1)} collective-permute-done((bf16[1024,384]{1,0:T(8,128)(2,1)S(1)}, bf16[1024,384]{1,0:T(8,128)(2,1)}, u32[]{:S(2)}, u32[]{:S(2)}) %collective-permute-start.7) | collective-permute-done | bytes 786464 | tf_op jit(solution)/shard_map/ppermute | solution.py:40
  92.5 1.7 fusion.52.q_ref
  94.2 9.0 %pad_maximum_fusion.1 = bf16[4096,384]{1,0:T(8,128)(2,1)S(1)} fusion(bf16[1024,384]{1,0:T(8,128)(2,1)S(1)} %collective-permute-done.8, bf16[1024,384]{1,0:T(8,128)(2,1)} %collective-permute-done.7, bf16[1024,384]{1,0:T(8,128)(2,1)S(1)} %collective-permute-done.6, bf16[1024,384]{1,0:T(8,128)(2,1)S(1)} %slice.301), kind=kLoop, calls=%fused_computation.8 | loop fusion | flops 12582912 | bytes 6291456 | tf_op jit(solution)/shard_map/concatenate | solution.py:321
  104.3 1.7 concatenate.118.v_ref
  106.0 2.1 maximum_maximum_fusion.k_ref
  108.1 22.0 %all-gather.3.cloned.1.call-done = bf16[1792,768]{1,0:T(8,128)(2,1)} async-done(((bf16[448,768]{1,0:T(8,128)(2,1)}), bf16[1792,768]{1,0:T(8,128)(2,1)}) %all-gather.3.cloned.1.call-update) | async-done | bytes 2752528 | tf_op jit(solution)/shard_map/all_gather | solution.py:310
  132.8 19.5 %attn_fwd.1 = (bf16[1024,256]{1,0:T(8,128)(2,1)}, f32[1024,128]{1,0:T(8,128)}) custom-call(bf16[1024,256]{1,0:T(8,128)(2,1)} %fusion.52.q_ref, bf16[4096,256]{1,0:T(8,128)(2,1)} %maximum_maximum_fusion.k_ref, bf16[4096,256]{1,0:T(8,128)(2,1)} %concatenate.118.v_ref), custom_call_target="tpu_custom_call" | custom-call | flops 12884901888 | bytes 5242880 | tf_op jit(solution)/shard_map/attn_fwd/pallas_call | solution.py:147
  152.3 2.0 copy.149
  154.3 3.9 all-to-all-start.1
  160.0 10.4 %all-to-all-done.1 = bf16[4,256,192]{1,2,0:T(8,128)(2,1)S(1)} async-done(((bf16[4,256,192]{1,2,0:T(8,128)(2,1)}), bf16[4,256,192]{1,2,0:T(8,128)(2,1)S(1)}, u32[]{:S(2)}, u32[]{:S(2)}) %all-to-all-start.1) | async-done | bytes 393248 | tf_op jit(solution)/shard_map/all_to_all | solution.py:336
  172.1 9.8 %collective-permute-done.13 = bf16[256,768]{1,0:T(8,128)(2,1)S(1)} collective-permute-done((bf16[256,768]{1,0:T(8,128)(2,1)S(1)}, bf16[256,768]{1,0:T(8,128)(2,1)S(1)}, u32[]{:S(2)}, u32[]{:S(2)}) %collective-permute-start.13) | collective-permute-done | bytes 393248 | tf_op jit(solution)/shard_map/ppermute | solution.py:40
  182.8 1.8 fusion.91
  184.6 11.6 %multiply_convert_fusion = (bf16[1024,768]{1,0:T(8,128)(2,1)S(1)}, f32[1024,768]{1,0:T(8,128)}, f32[1024,768]{1,0:T(8,128)}) fusion(f32[768]{0:T(1024)S(1)} %add.354, bf16[768,768]{1,0:T(8,128)(2,1)S(1)} %bitcast.241, bf16[256,768]{1,0:T(8,128)(2,1)} %collective-permute-done.14, bf16[256,768]{1,0:T(8,128)(2,1)S(1)} %collective-permute-done.13, ...), kind=kOutput, calls=%fused_computation.11 | convolution fusion | flops 1266155520 | bytes 10619904 | tf_op jit(solution)/shard_map/dot_general | solution.py:28
  198.3 1.9 collective-permute-done.15
  203.2 9.6 %collective-permute-done.16 = bf16[256,768]{1,0:T(8,128)(2,1)} collective-permute-done((bf16[256,768]{1,0:T(8,128)(2,1)S(1)}, bf16[256,768]{1,0:T(8,128)(2,1)}, u32[]{:S(2)}, u32[]{:S(2)}) %collective-permute-start.16) | collective-permute-done | bytes 393248 | tf_op jit(solution)/shard_map/ppermute | solution.py:40
  212.8 1.8 fusion.87
  217.3 10.0 %collective-permute-done.18 = bf16[256,768]{1,0:T(8,128)(2,1)S(1)} collective-permute-done((bf16[256,768]{1,0:T(8,128)(2,1)S(1)}, bf16[256,768]{1,0:T(8,128)(2,1)S(1)}, u32[]{:S(2)}, u32[]{:S(2)}) %collective-permute-start.18) | collective-permute-done | bytes 393248 | tf_op jit(solution)/shard_map/ppermute | solution.py:40
  227.4 1.7 collective-permute-done.19
  229.1 6.2 %convert_reduce_fusion = (f32[768]{0:T(1024)}, bf16[1024,768]{1,0:T(8,128)(2,1)S(1)}) fusion(f32[1024,768]{1,0:T(8,128)S(1)} %copy-done.68, bf16[768,768]{1,0:T(8,128)(2,1)S(1)} %bitcast.244, bf16[256,768]{1,0:T(8,128)(2,1)S(1)} %collective-permute-done.19, bf16[256,768]{1,0:T(8,128)(2,1)S(1)} %collective-permute-done.18, ...), kind=kOutput, calls=%fused_computation.9 | convolution fusion | flops 1227619584 | bytes 10622976 | tf_op jit(solution)/shard_map/dot_general | solution.py:28
  235.4 3.0 fusion.98
  242.1 2.1 fusion.61
  244.2 1.8 copy.154
  245.9 1.8 copy.156
  247.7 1.8 copy.155
  252.2 1.6 copy.157
  255.8 4.3 convolution_convert_fusion
  260.1 6.5 %collective-permute-done.21 = bf16[256,768]{1,0:T(8,128)(2,1)S(1)} collective-permute-done((bf16[256,768]{1,0:T(8,128)(2,1)S(1)}, bf16[256,768]{1,0:T(8,128)(2,1)S(1)}, u32[]{:S(2)}, u32[]{:S(2)}) %collective-permute-start.21) | collective-permute-done | bytes 393248 | tf_op jit(solution)/shard_map/ppermute | solution.py:40
  266.7 3.4 multiply_reduce_fusion.1
  271.9 4.1 all-to-all-start.3
  276.1 4.1 convolution_convert_fusion.1
  281.6 6.2 %all-to-all-done.3 = bf16[256,4,192]{0,2,1:T(8,128)(2,1)} async-done(((bf16[256,4,192]{0,2,1:T(8,128)(2,1)}), bf16[256,4,192]{0,2,1:T(8,128)(2,1)}, u32[]{:S(2)}, u32[]{:S(2)}) %all-to-all-start.3) | async-done | bytes 393248 | tf_op jit(solution)/shard_map/all_to_all | solution.py:369
  287.8 2.0 copy.159
  289.8 2.3 convert_multiply_fusion
  292.1 2.5 copy.160
  296.7 1.7 fusion.47
  299.0 2.7 maximum_maximum_fusion.2
  301.7 37.6 %attn_bwd.1 = (f32[1024,256]{1,0:T(8,128)}, f32[4096,256]{1,0:T(8,128)}, f32[4096,256]{1,0:T(8,128)}) custom-call(bf16[1024,256]{1,0:T(8,128)(2,1)} %get-tuple-element.99.q_ref, bf16[1024,256]{1,0:T(8,128)(2,1)} %get-tuple-element.98.do_ref, bf16[4096,256]{1,0:T(8,128)(2,1)} %maximum_maximum_fusion.k_ref, bf16[4096,256]{1,0:T(8,128)(2,1)} %concatenate.118.v_ref), custom_call_target="tpu_custom_call" | custom-call | flops 32212254720 | bytes 10485760 | tf_op jit(solution)/shard_map/attn_bwd/pallas_call | solution.py:209
  339.3 4.4 fusion
  346.3 1.6 pad_maximum_fusion.2
  348.9 3.0 fusion.29
  353.5 1.6 copy.165
  355.8 16.1 %collective-permute-done.23 = bf16[1024,384]{1,0:T(8,128)(2,1)} collective-permute-done((bf16[1024,384]{1,0:T(8,128)(2,1)}, bf16[1024,384]{1,0:T(8,128)(2,1)}, u32[]{:S(2)}, u32[]{:S(2)}) %collective-permute-start.23) | collective-permute-done | bytes 786464 | tf_op jit(solution)/shard_map/ppermute | solution.py:40
  372.0 2.5 fusion.26
  380.3 18.9 %collective-permute-done.24 = bf16[256,768]{1,0:T(8,128)(2,1)S(1)} collective-permute-done((bf16[256,768]{1,0:T(8,128)(2,1)S(1)}, bf16[256,768]{1,0:T(8,128)(2,1)S(1)}, u32[]{:S(2)}, u32[]{:S(2)}) %collective-permute-start.24) | collective-permute-done | bytes 393248 | tf_op jit(solution)/shard_map/ppermute | solution.py:45
  400.0 4.3 collective-permute-start.25
  407.4 2.8 collective-permute-done.31
  413.1 4.0 collective-permute-done.25
  417.1 2.1 fusion.41
  422.1 9.1 %collective-permute-done.33 = f32[12,768]{1,0:T(8,128)S(1)} collective-permute-done((f32[12,768]{1,0:T(8,128)S(1)}, f32[12,768]{1,0:T(8,128)S(1)}, u32[]{:S(2)}, u32[]{:S(2)}) %collective-permute-start.33) | collective-permute-done | bytes 36896 | tf_op jit(solution)/shard_map/ppermute | solution.py:426
  431.2 2.2 collective-permute-start.34
  433.4 2.9 collective-permute-done.34
  439.7 3.4 all-to-all-start.4
  443.8 2.2 fusion.42
  446.0 3.7 all-to-all-done.4
  455.5 3.5 all-to-all-start.5
  459.6 6.7 %all-to-all-done.5 = bf16[192,4,192]{2,0,1:T(8,128)(2,1)S(1)} async-done(((bf16[192,4,192]{2,0,1:T(8,128)(2,1)}), bf16[192,4,192]{2,0,1:T(8,128)(2,1)S(1)}, u32[]{:S(2)}, u32[]{:S(2)}) %all-to-all-start.5) | async-done | bytes 294944 | tf_op jit(solution)/shard_map/all_to_all | solution.py:378
  (364 shorter events, 86.1 us)
Async XLA Ops:
  7.2 14.0 %copy-start.55 = (f32[192]{0:T(256)S(1)}, f32[192]{0:T(256)}, u32[]{:S(2)}) copy-start(f32[192]{0:T(256)} %param.35) | copy-start | bytes 2308
  7.2 14.0 %copy-start.54 = (f32[192]{0:T(256)S(1)}, f32[192]{0:T(256)}, u32[]{:S(2)}) copy-start(f32[192]{0:T(256)} %param.34) | copy-start | bytes 2308
  7.2 14.0 %copy-start.53 = (f32[192]{0:T(256)S(1)}, f32[192]{0:T(256)}, u32[]{:S(2)}) copy-start(f32[192]{0:T(256)} %param.33) | copy-start | bytes 2308
  7.2 14.0 %copy-start.52 = (f32[192]{0:T(256)S(1)}, f32[192]{0:T(256)}, u32[]{:S(2)}) copy-start(f32[192]{0:T(256)} %param.29) | copy-start | bytes 2308
  7.2 14.0 %copy-start.51 = (f32[192]{0:T(256)S(1)}, f32[192]{0:T(256)}, u32[]{:S(2)}) copy-start(f32[192]{0:T(256)} %param.28) | copy-start | bytes 2308
  7.3 14.0 %copy-start.50 = (f32[192]{0:T(256)S(1)}, f32[192]{0:T(256)}, u32[]{:S(2)}) copy-start(f32[192]{0:T(256)} %param.27) | copy-start | bytes 2308
  7.3 14.0 %copy-start.22 = (f32[192,768]{1,0:T(8,128)S(1)}, f32[192,768]{1,0:T(8,128)}, u32[]{:S(2)}) copy-start(f32[192,768]{1,0:T(8,128)} %param.30) | copy-start | bytes 1769476
  8.3 14.7 %copy-start.27 = (f32[48,768]{1,0:T(8,128)S(1)}, f32[48,768]{1,0:T(8,128)}, u32[]{:S(2)}) copy-start(f32[48,768]{1,0:T(8,128)} %param.26) | copy-start | bytes 442372
  10.9 13.8 %copy-start.56 = (f32[192]{0:T(256)S(1)}, f32[192]{0:T(256)}, u32[]{:S(2)}) copy-start(f32[192]{0:T(256)} %param.25) | copy-start | bytes 2308
  10.9 13.8 %copy-start.57 = (f32[192]{0:T(256)S(1)}, f32[192]{0:T(256)}, u32[]{:S(2)}) copy-start(f32[192]{0:T(256)} %param.24) | copy-start | bytes 2308
  12.9 23.3 %all-to-all-start = ((bf16[4,48,576]{2,1,0:T(8,128)(2,1)}), bf16[4,48,576]{2,1,0:T(8,128)(2,1)S(1)}, u32[]{:S(2)}, u32[]{:S(2)}) async-start(bf16[4,48,576]{2,1,0:T(8,128)(2,1)} %reshape.736), calls=%async_computation | async-start | bytes 491520 | tf_op jit(solution)/shard_map/all_to_all | solution.py:287
  19.2 16.6 %collective-permute-start = (bf16[256,768]{1,0:T(8,128)(2,1)S(1)}, bf16[256,768]{1,0:T(8,128)(2,1)S(1)}, u32[]{:S(2)}, u32[]{:S(2)}) collective-permute-start(bf16[256,768]{1,0:T(8,128)(2,1)S(1)} %copy-done.6), channel_id=1, source_target_pairs={{0,1},{1,2},{2,3},{3,0},{4,5},{5,6},{6,7},{7,4},{8,9},{9,10},{10,1... | collective-permute-start | bytes 1179656 | tf_op jit(solution)/shard_map/ppermute | solution.py:45
  35.8 17.8 %collective-permute-start.1 = (bf16[256,768]{1,0:T(8,128)(2,1)S(1)}, bf16[256,768]{1,0:T(8,128)(2,1)}, u32[]{:S(2)}, u32[]{:S(2)}) collective-permute-start(bf16[256,768]{1,0:T(8,128)(2,1)S(1)} %collective-permute-done), channel_id=1, source_target_pairs={{0,1},{1,2},{2,3},{3,0},{4,5},{5,6},{6,7},{7,4},{8,9},{9,10},{10,1... | collective-permute-start | bytes 1179656 | tf_op jit(solution)/shard_map/ppermute | solution.py:45
  36.2 33.9 %all-to-all-start.2 = ((bf16[4,192,192]{2,1,0:T(8,128)(2,1)}), bf16[4,192,192]{2,1,0:T(8,128)(2,1)}, u32[]{:S(2)}, u32[]{:S(2)}) async-start(bf16[4,192,192]{2,1,0:T(8,128)(2,1)} %bitcast.23), calls=%async_computation.2 | async-start | bytes 786432 | tf_op jit(solution)/shard_map/all_to_all | solution.py:304
  40.3 89.9 %all-gather.3.cloned.1.call-start = ((), (), s32[]{:S(2)}) async-start(), calls=%async_computation.8 | async-start | bytes 3440640 | tf_op jit(solution)/shard_map/all_gather | solution.py:310
  40.4 13.0 %collective-permute-start.3 = (bf16[208,576]{1,0:T(8,128)(2,1)S(1)}, bf16[208,576]{1,0:T(8,128)(2,1)S(1)}, u32[]{:S(2)}, u32[]{:S(2)}) collective-permute-start(bf16[208,576]{1,0:T(8,128)(2,1)S(1)} %get-tuple-element.78), channel_id=1, source_target_pairs={{0,4},{4,0},{8,12},{12,8},{1,5},{5,1},{9,13},{13,9},{2,6},{6,2},{1... | collective-permute-start | bytes 718856 | tf_op jit(solution)/shard_map/ppermute | solution.py:36
  40.9 12.5 %collective-permute-start.4 = (bf16[208,576]{1,0:T(8,128)(2,1)S(1)}, bf16[208,576]{1,0:T(8,128)(2,1)S(1)}, u32[]{:S(2)}, u32[]{:S(2)}) collective-permute-start(bf16[208,576]{1,0:T(8,128)(2,1)S(1)} %get-tuple-element.78), channel_id=1, source_target_pairs={{0,8},{8,0},{4,12},{12,4},{1,9},{9,1},{5,13},{13,5},{2,10},{10,2},... | collective-permute-start | bytes 718856 | tf_op jit(solution)/shard_map/ppermute | solution.py:40
  53.4 2.4 collective-permute-start.5
  53.6 13.6 %collective-permute-start.2 = (bf16[256,768]{1,0:T(8,128)(2,1)}, bf16[256,768]{1,0:T(8,128)(2,1)S(1)}, u32[]{:S(2)}, u32[]{:S(2)}) collective-permute-start(bf16[256,768]{1,0:T(8,128)(2,1)} %collective-permute-done.1), channel_id=1, source_target_pairs={{0,1},{1,2},{2,3},{3,0},{4,5},{5,6},{6,7},{7,4},{8,9},{9,10},{10,1... | collective-permute-start | bytes 1179656 | tf_op jit(solution)/shard_map/ppermute | solution.py:45
  69.7 19.3 %collective-permute-start.7 = (bf16[1024,384]{1,0:T(8,128)(2,1)S(1)}, bf16[1024,384]{1,0:T(8,128)(2,1)}, u32[]{:S(2)}, u32[]{:S(2)}) collective-permute-start(bf16[1024,384]{1,0:T(8,128)(2,1)S(1)} %slice.301), channel_id=1, source_target_pairs={{0,8},{8,0},{4,12},{12,4},{1,9},{9,1},{5,13},{13,5},{2,10},{10,2},... | collective-permute-start | bytes 2359304 | tf_op jit(solution)/shard_map/ppermute | solution.py:40
  76.4 17.8 %collective-permute-start.6 = (bf16[1024,384]{1,0:T(8,128)(2,1)S(1)}, bf16[1024,384]{1,0:T(8,128)(2,1)S(1)}, u32[]{:S(2)}, u32[]{:S(2)}) collective-permute-start(bf16[1024,384]{1,0:T(8,128)(2,1)S(1)} %slice.301), channel_id=1, source_target_pairs={{0,4},{4,0},{8,12},{12,8},{1,5},{5,1},{9,13},{13,9},{2,6},{6,2},{1... | collective-permute-start | bytes 2359304 | tf_op jit(solution)/shard_map/ppermute | solution.py:36
  88.9 5.2 %collective-permute-start.8 = (bf16[1024,384]{1,0:T(8,128)(2,1)}, bf16[1024,384]{1,0:T(8,128)(2,1)S(1)}, u32[]{:S(2)}, u32[]{:S(2)}) collective-permute-start(bf16[1024,384]{1,0:T(8,128)(2,1)} %collective-permute-done.7), channel_id=1, source_target_pairs={{0,4},{4,0},{8,12},{12,8},{1,5},{5,1},{9,13},{13,9},{2,6},{6,2},{1... | collective-permute-start | bytes 2359304 | tf_op jit(solution)/shard_map/ppermute | solution.py:36
  131.2 27.3 %collective-permute-start.9 = (bf16[4,48,768]{2,1,0:T(8,128)(2,1)S(1)}, bf16[4,48,768]{2,1,0:T(8,128)(2,1)S(1)}, u32[]{:S(2)}, u32[]{:S(2)}) collective-permute-start(bf16[4,48,768]{2,1,0:T(8,128)(2,1)S(1)} %get-tuple-element.57), channel_id=1, source_target_pairs={{0,4},{4,0},{8,12},{12,8},{1,5},{5,1},{9,13},{13,9},{2,6},{6,2},{1... | collective-permute-start | bytes 884744 | tf_op jit(solution)/shard_map/ppermute | solution.py:36
  131.2 26.9 %collective-permute-start.10 = (bf16[4,48,768]{2,1,0:T(8,128)(2,1)S(1)}, bf16[4,48,768]{2,1,0:T(8,128)(2,1)S(1)}, u32[]{:S(2)}, u32[]{:S(2)}) collective-permute-start(bf16[4,48,768]{2,1,0:T(8,128)(2,1)S(1)} %get-tuple-element.57), channel_id=1, source_target_pairs={{0,8},{8,0},{4,12},{12,4},{1,9},{9,1},{5,13},{13,5},{2,10},{10,2},... | collective-permute-start | bytes 884744 | tf_op jit(solution)/shard_map/ppermute | solution.py:40
  154.3 16.1 %all-to-all-start.1 = ((bf16[4,256,192]{1,2,0:T(8,128)(2,1)}), bf16[4,256,192]{1,2,0:T(8,128)(2,1)S(1)}, u32[]{:S(2)}, u32[]{:S(2)}) async-start(bf16[4,256,192]{1,2,0:T(8,128)(2,1)} %copy.149), calls=%async_computation.1 | async-start | bytes 786432 | tf_op jit(solution)/shard_map/all_to_all | solution.py:336
  158.2 1.6 collective-permute-start.11
  171.5 24.7 %copy-start.24 = (bf16[256,768]{1,0:T(8,128)(2,1)}, bf16[256,768]{1,0:T(8,128)(2,1)S(1)}, u32[]{:S(2)}) copy-start(bf16[256,768]{1,0:T(8,128)(2,1)S(1)} %fusion.46) | copy-start | bytes 1179652
  171.5 10.4 %collective-permute-start.13 = (bf16[256,768]{1,0:T(8,128)(2,1)S(1)}, bf16[256,768]{1,0:T(8,128)(2,1)S(1)}, u32[]{:S(2)}, u32[]{:S(2)}) collective-permute-start(bf16[256,768]{1,0:T(8,128)(2,1)S(1)} %fusion.46), channel_id=1, source_target_pairs={{0,8},{8,0},{4,12},{12,4},{1,9},{9,1},{5,13},{13,5},{2,10},{10,2},... | collective-permute-start | bytes 1179656 | tf_op jit(solution)/shard_map/ppermute | solution.py:40
  172.1 12.5 %collective-permute-start.12 = (bf16[256,768]{1,0:T(8,128)(2,1)S(1)}, bf16[256,768]{1,0:T(8,128)(2,1)}, u32[]{:S(2)}, u32[]{:S(2)}) collective-permute-start(bf16[256,768]{1,0:T(8,128)(2,1)S(1)} %fusion.46), channel_id=1, source_target_pairs={{0,4},{4,0},{8,12},{12,8},{1,5},{5,1},{9,13},{13,9},{2,6},{6,2},{1... | collective-permute-start | bytes 1179656 | tf_op jit(solution)/shard_map/ppermute | solution.py:36
  181.9 14.3 %copy-start.61 = (bf16[256,768]{1,0:T(8,128)(2,1)}, bf16[256,768]{1,0:T(8,128)(2,1)S(1)}, u32[]{:S(2)}) copy-start(bf16[256,768]{1,0:T(8,128)(2,1)S(1)} %collective-permute-done.13) | copy-start | bytes 1179652
  181.9 2.7 collective-permute-start.14
  197.8 2.5 collective-permute-start.15
  201.2 11.6 %collective-permute-start.16 = (bf16[256,768]{1,0:T(8,128)(2,1)S(1)}, bf16[256,768]{1,0:T(8,128)(2,1)}, u32[]{:S(2)}, u32[]{:S(2)}) collective-permute-start(bf16[256,768]{1,0:T(8,128)(2,1)S(1)} %fusion.36), channel_id=1, source_target_pairs={{0,8},{8,0},{4,12},{12,4},{1,9},{9,1},{5,13},{13,5},{2,10},{10,2},... | collective-permute-start | bytes 1179656 | tf_op jit(solution)/shard_map/ppermute | solution.py:40
  203.2 25.9 %copy-start.13 = (bf16[4,192,768]{2,1,0:T(8,128)(2,1)S(1)}, bf16[4,192,768]{2,1,0:T(8,128)(2,1)}, u32[]{:S(2)}) copy-start(bf16[4,192,768]{2,1,0:T(8,128)(2,1)} %copy-done.12) | copy-start | bytes 3538948
  203.2 25.9 %copy-start.48 = (f32[768]{0:T(1024)S(1)}, f32[768]{0:T(1024)}, u32[]{:S(2)}) copy-start(f32[768]{0:T(1024)} %copy-done.47) | copy-start | bytes 9220
  203.2 25.9 %copy-start.68 = (f32[1024,768]{1,0:T(8,128)S(1)}, f32[1024,768]{1,0:T(8,128)}, u32[]{:S(2)}) copy-start(f32[1024,768]{1,0:T(8,128)} %get-tuple-element.49) | copy-start | bytes 9437188
  214.8 14.2 %copy-start.40 = (f32[256]{0:T(256)}, f32[256]{0:T(256)S(1)}, u32[]{:S(2)}) copy-start(f32[256]{0:T(256)S(1)} %add_rsqrt_fusion) | copy-start | bytes 3076
  216.8 18.6 %copy-start.26 = (bf16[256,768]{1,0:T(8,128)(2,1)}, bf16[256,768]{1,0:T(8,128)(2,1)S(1)}, u32[]{:S(2)}) copy-start(bf16[256,768]{1,0:T(8,128)(2,1)S(1)} %get-tuple-element.44) | copy-start | bytes 1179652
  216.8 10.6 %collective-permute-start.18 = (bf16[256,768]{1,0:T(8,128)(2,1)S(1)}, bf16[256,768]{1,0:T(8,128)(2,1)S(1)}, u32[]{:S(2)}, u32[]{:S(2)}) collective-permute-start(bf16[256,768]{1,0:T(8,128)(2,1)S(1)} %get-tuple-element.44), channel_id=1, source_target_pairs={{0,8},{8,0},{4,12},{12,4},{1,9},{9,1},{5,13},{13,5},{2,10},{10,2},... | collective-permute-start | bytes 1179656 | tf_op jit(solution)/shard_map/ppermute | solution.py:40
  217.3 10.0 %collective-permute-start.17 = (bf16[256,768]{1,0:T(8,128)(2,1)S(1)}, bf16[256,768]{1,0:T(8,128)(2,1)S(1)}, u32[]{:S(2)}, u32[]{:S(2)}) collective-permute-start(bf16[256,768]{1,0:T(8,128)(2,1)S(1)} %get-tuple-element.44), channel_id=1, source_target_pairs={{0,4},{4,0},{8,12},{12,8},{1,5},{5,1},{9,13},{13,9},{2,6},{6,2},{1... | collective-permute-start | bytes 1179656 | tf_op jit(solution)/shard_map/ppermute | solution.py:36
  227.3 1.7 collective-permute-start.19
  239.4 14.4 %collective-permute-start.20 = (bf16[2,256,768]{2,1,0:T(8,128)(2,1)}, bf16[2,256,768]{2,1,0:T(8,128)(2,1)}, u32[]{:S(2)}, u32[]{:S(2)}) collective-permute-start(bf16[2,256,768]{2,1,0:T(8,128)(2,1)} %pad_maximum_fusion.8), channel_id=1, source_target_pairs={{0,4},{4,0},{8,12},{12,8},{1,5},{5,1},{9,13},{13,9},{2,6},{6,2},{1... | collective-permute-start | bytes 2359304 | tf_op jit(solution)/shard_map/ppermute | solution.py:36
  255.2 11.5 %collective-permute-start.21 = (bf16[256,768]{1,0:T(8,128)(2,1)S(1)}, bf16[256,768]{1,0:T(8,128)(2,1)S(1)}, u32[]{:S(2)}, u32[]{:S(2)}) collective-permute-start(bf16[256,768]{1,0:T(8,128)(2,1)S(1)} %fusion.33), channel_id=1, source_target_pairs={{0,8},{8,0},{4,12},{12,4},{1,9},{9,1},{5,13},{13,5},{2,10},{10,2},... | collective-permute-start | bytes 1179656 | tf_op jit(solution)/shard_map/ppermute | solution.py:40
  271.9 15.9 %all-to-all-start.3 = ((bf16[256,4,192]{0,2,1:T(8,128)(2,1)}), bf16[256,4,192]{0,2,1:T(8,128)(2,1)}, u32[]{:S(2)}, u32[]{:S(2)}) async-start(bf16[256,4,192]{0,2,1:T(8,128)(2,1)} %bitcast.47), calls=%async_computation.3 | async-start | bytes 786432 | tf_op jit(solution)/shard_map/all_to_all | solution.py:369
  276.0 160.3 %reduce-scatter.2.cloned.1.call-start = ((), (), s32[]{:S(2)}) async-start(), calls=%async_computation.7 | async-start | bytes 3317760 | tf_op jit(solution)/shard_map/reduce_scatter | solution.py:375
  281.6 15.1 %collective-permute-start.35 = (bf16[2,4,48,768]{3,2,1,0:T(8,128)(2,1)}, bf16[2,4,48,768]{3,2,1,0:T(8,128)(2,1)}, u32[]{:S(2)}, u32[]{:S(2)}) collective-permute-start(bf16[2,4,48,768]{3,2,1,0:T(8,128)(2,1)} %pad_maximum_fusion.12), channel_id=1, source_target_pairs={{0,4},{4,0},{8,12},{12,8},{1,5},{5,1},{9,13},{13,9},{2,6},{6,2},{1... | collective-permute-start | bytes 1769480 | tf_op jit(solution)/shard_map/ppermute | solution.py:36
  298.4 46.8 %collective-permute-start.36 = (bf16[4,48,768]{2,1,0:T(8,128)(2,1)}, bf16[4,48,768]{2,1,0:T(8,128)(2,1)S(1)}, u32[]{:S(2)}, u32[]{:S(2)}) collective-permute-start(bf16[4,48,768]{2,1,0:T(8,128)(2,1)} %fusion.47), channel_id=1, source_target_pairs={{0,8},{8,0},{4,12},{12,4},{1,9},{9,1},{5,13},{13,5},{2,10},{10,2},... | collective-permute-start | bytes 884744 | tf_op jit(solution)/shard_map/ppermute | solution.py:40
  345.2 3.8 collective-permute-start.22
  352.0 20.0 %collective-permute-start.23 = (bf16[1024,384]{1,0:T(8,128)(2,1)}, bf16[1024,384]{1,0:T(8,128)(2,1)}, u32[]{:S(2)}, u32[]{:S(2)}) collective-permute-start(bf16[1024,384]{1,0:T(8,128)(2,1)} %fusion.29), channel_id=1, source_target_pairs={{0,8},{8,0},{4,12},{12,4},{1,9},{9,1},{5,13},{13,5},{2,10},{10,2},... | collective-permute-start | bytes 2359304 | tf_op jit(solution)/shard_map/ppermute | solution.py:40
  377.1 22.1 %copy-start.4 = (f32[4,256,768]{2,1,0:T(8,128)}, f32[4,256,768]{2,1,0:T(8,128)S(1)}, u32[]{:S(2)}) copy-start(f32[4,256,768]{2,1,0:T(8,128)S(1)} %fusion.99) | copy-start | bytes 9437188
  377.2 22.0 %collective-permute-start.24 = (bf16[256,768]{1,0:T(8,128)(2,1)S(1)}, bf16[256,768]{1,0:T(8,128)(2,1)S(1)}, u32[]{:S(2)}, u32[]{:S(2)}) collective-permute-start(bf16[256,768]{1,0:T(8,128)(2,1)S(1)} %fusion.53), channel_id=1, source_target_pairs={{0,1},{1,2},{2,3},{3,0},{4,5},{5,6},{6,7},{7,4},{8,9},{9,10},{10,1... | collective-permute-start | bytes 1179656 | tf_op jit(solution)/shard_map/ppermute | solution.py:45
  379.7 31.9 %collective-permute-start.27 = (bf16[2,192,576]{2,1,0:T(8,128)(2,1)}, bf16[2,192,576]{2,1,0:T(8,128)(2,1)S(1)}, u32[]{:S(2)}, u32[]{:S(2)}) collective-permute-start(bf16[2,192,576]{2,1,0:T(8,128)(2,1)} %pad_maximum_fusion.14), channel_id=1, source_target_pairs={{0,4},{4,0},{8,12},{12,8},{1,5},{5,1},{9,13},{13,9},{2,6},{6,2},{1... | collective-permute-start | bytes 1327112 | tf_op jit(solution)/shard_map/ppermute | solution.py:36
  400.0 17.1 %collective-permute-start.25 = (bf16[256,768]{1,0:T(8,128)(2,1)}, bf16[256,768]{1,0:T(8,128)(2,1)}, u32[]{:S(2)}, u32[]{:S(2)}) collective-permute-start(bf16[256,768]{1,0:T(8,128)(2,1)} %fusion.40), channel_id=1, source_target_pairs={{0,1},{1,2},{2,3},{3,0},{4,5},{5,6},{6,7},{7,4},{8,9},{9,10},{10,1... | collective-permute-start | bytes 1179656 | tf_op jit(solution)/shard_map/ppermute | solution.py:45
  404.7 1.3 collective-permute-start.30
  406.0 4.2 collective-permute-start.31
  410.2 10.6 %collective-permute-start.32 = (f32[12,768]{1,0:T(8,128)S(1)}, f32[12,768]{1,0:T(8,128)S(1)}, u32[]{:S(2)}, u32[]{:S(2)}) collective-permute-start(f32[12,768]{1,0:T(8,128)S(1)} %add.395), channel_id=1, source_target_pairs={{0,16},{16,0},{1,17},{17,1},{2,18},{18,2},{3,19},{19,3},{4,20},{20... | collective-permute-start | bytes 110600 | tf_op jit(solution)/shard_map/ppermute | solution.py:98
  411.6 7.6 %collective-permute-start.28 = (bf16[192,576]{1,0:T(8,128)(2,1)S(1)}, bf16[192,576]{1,0:T(8,128)(2,1)S(1)}, u32[]{:S(2)}, u32[]{:S(2)}) collective-permute-start(bf16[192,576]{1,0:T(8,128)(2,1)S(1)} %fusion.63), channel_id=1, source_target_pairs={{0,8},{8,0},{4,12},{12,4},{1,9},{9,1},{5,13},{13,5},{2,10},{10,2},... | collective-permute-start | bytes 663560 | tf_op jit(solution)/shard_map/ppermute | solution.py:40
  419.2 24.6 %collective-permute-start.26 = (bf16[256,768]{1,0:T(8,128)(2,1)}, bf16[256,768]{1,0:T(8,128)(2,1)}, u32[]{:S(2)}, u32[]{:S(2)}) collective-permute-start(bf16[256,768]{1,0:T(8,128)(2,1)} %fusion.41), channel_id=1, source_target_pairs={{0,1},{1,2},{2,3},{3,0},{4,5},{5,6},{6,7},{7,4},{8,9},{9,10},{10,1... | collective-permute-start | bytes 1179656 | tf_op jit(solution)/shard_map/ppermute | solution.py:45
  419.3 19.7 %collective-permute-start.29 = (bf16[192,576]{1,0:T(8,128)(2,1)S(1)}, bf16[192,576]{1,0:T(8,128)(2,1)S(1)}, u32[]{:S(2)}, u32[]{:S(2)}) collective-permute-start(bf16[192,576]{1,0:T(8,128)(2,1)S(1)} %fusion.51), channel_id=1, source_target_pairs={{0,16},{16,0},{1,17},{17,1},{2,18},{18,2},{3,19},{19,3},{4,20},{20... | collective-permute-start | bytes 663560 | tf_op jit(solution)/shard_map/ppermute | solution.py:98
  420.8 10.4 %collective-permute-start.33 = (f32[12,768]{1,0:T(8,128)S(1)}, f32[12,768]{1,0:T(8,128)S(1)}, u32[]{:S(2)}, u32[]{:S(2)}) collective-permute-start(f32[12,768]{1,0:T(8,128)S(1)} %add.396), channel_id=1, source_target_pairs={{0,1},{1,0},{2,3},{3,2},{4,5},{5,4},{6,7},{7,6},{8,9},{9,8},{10,11... | collective-permute-start | bytes 110600 | tf_op jit(solution)/shard_map/ppermute | solution.py:426
  431.2 5.0 %collective-permute-start.34 = (f32[12,768]{1,0:T(8,128)S(1)}, f32[12,768]{1,0:T(8,128)S(1)}, u32[]{:S(2)}, u32[]{:S(2)}) collective-permute-start(f32[12,768]{1,0:T(8,128)S(1)} %add.397), channel_id=1, source_target_pairs={{0,2},{1,3},{2,0},{3,1},{4,6},{5,7},{6,4},{7,5},{8,10},{9,11},{10,... | collective-permute-start | bytes 110600 | tf_op jit(solution)/shard_map/ppermute | solution.py:427
  436.3 17.0 %collective-permute-start.37 = (bf16[432,768]{1,0:T(8,128)(2,1)}, bf16[432,768]{1,0:T(8,128)(2,1)S(1)}, u32[]{:S(2)}, u32[]{:S(2)}) collective-permute-start(bf16[432,768]{1,0:T(8,128)(2,1)} %bitcast.249), channel_id=1, source_target_pairs={{0,16},{16,0},{1,17},{17,1},{2,18},{18,2},{3,19},{19,3},{4,20},{20... | collective-permute-start | bytes 1990664 | tf_op jit(solution)/shard_map/ppermute | solution.py:98
  439.7 10.0 %all-to-all-start.4 = ((bf16[4,48,576]{2,1,0:T(8,128)(2,1)}), bf16[4,48,576]{2,1,0:T(8,128)(2,1)S(1)}, u32[]{:S(2)}, u32[]{:S(2)}) async-start(bf16[4,48,576]{2,1,0:T(8,128)(2,1)} %bitcast.67), calls=%async_computation.4 | async-start | bytes 491520 | tf_op jit(solution)/shard_map/all_to_all | solution.py:406
  455.5 10.9 %all-to-all-start.5 = ((bf16[192,4,192]{2,0,1:T(8,128)(2,1)}), bf16[192,4,192]{2,0,1:T(8,128)(2,1)S(1)}, u32[]{:S(2)}, u32[]{:S(2)}) async-start(bf16[192,4,192]{2,0,1:T(8,128)(2,1)} %copy.171), calls=%async_computation.6 | async-start | bytes 786432 | tf_op jit(solution)/shard_map/all_to_all | solution.py:378
  (51 other events, 357.5 us)
Sparse Core Ops, SparseCore 0:
  73.7 56.4 all-gather.2
  348.1 60.0 reduce-scatter.1
